TPU v7x, 32 devices: a whole 2x2x4 slice. The times are simulated.
32 devices in a mesh: dp: 4 (over x, core), fsdp: 8 (over z, y).
Axes of the slice: x: 2, y: 2, z: 4, core: 2. Of those that a mesh axis runs over, the one named last changes fastest.
Arguments:
- tokens: bfloat16 [16384, 768], P(('dp', 'fsdp')), may hold values from -6 to 6
- cotangent: bfloat16 [16384, 768], P(('dp', 'fsdp')), may hold values from -6 to 6
- tile_dest: int32 [128], P(('dp', 'fsdp')), may hold values from 0 to 31, as said below
- seq_lengths: int32 [32, 4], P(('dp', 'fsdp')), may hold values from 0 to 512, as said below
- norm1_gain: float32 [768], P(('dp', 'fsdp')), may hold values from 0.5 to 1.5
- norm1_bias: float32 [768], P(('dp', 'fsdp')), may hold values from -1.5 to 1.5
- w_qkv: float32 [768, 2304], P(('dp', 'fsdp')), may hold values from -0.3125 to 0.3125
- q_bias: float32 [768], P(('dp', 'fsdp')), may hold values from -1.5 to 1.5
- v_bias: float32 [768], P(('dp', 'fsdp')), may hold values from -1.5 to 1.5
- w_out: float32 [768, 768], P(('dp', 'fsdp')), may hold values from -0.75 to 0.75
- out_bias: float32 [768], P(('dp', 'fsdp')), may hold values from -1.5 to 1.5
- norm2_gain: float32 [768], P(('dp', 'fsdp')), may hold values from 0.5 to 1.5
- norm2_bias: float32 [768], P(('dp', 'fsdp')), may hold values from -1.5 to 1.5
- w_up: float32 [768, 3072], P(('dp', 'fsdp')), may hold values from -0.21875 to 0.21875
- up_bias: float32 [3072], P(('dp', 'fsdp')), may hold values from -1.5 to 1.5
- w_down: float32 [3072, 768], P(('dp', 'fsdp')), may hold values from -0.109375 to 0.109375
- down_bias: float32 [768], P(('dp', 'fsdp')), may hold values from -1.5 to 1.5
Outputs:
- mixed: bfloat16 [16384, 768], P(('dp', 'fsdp'))
- grad_tokens: bfloat16 [16384, 768], P(('dp', 'fsdp'))
- grad_norm1_gain: float32 [768], P(('dp', 'fsdp'))
- grad_norm1_bias: float32 [768], P(('dp', 'fsdp'))
- grad_w_qkv: float32 [768, 2304], P(('dp', 'fsdp'))
- grad_q_bias: float32 [768], P(('dp', 'fsdp'))
- grad_v_bias: float32 [768], P(('dp', 'fsdp'))
- grad_w_out: float32 [768, 768], P(('dp', 'fsdp'))
- grad_out_bias: float32 [768], P(('dp', 'fsdp'))
- grad_norm2_gain: float32 [768], P(('dp', 'fsdp'))
- grad_norm2_bias: float32 [768], P(('dp', 'fsdp'))
- grad_w_up: float32 [768, 3072], P(('dp', 'fsdp'))
- grad_up_bias: float32 [3072], P(('dp', 'fsdp'))
- grad_w_down: float32 [3072, 768], P(('dp', 'fsdp'))
- grad_down_bias: float32 [768], P(('dp', 'fsdp'))
Inputs may be any that keep to these rules, and one draw needn't show every extreme that they name: `tile_dest`: within each dp index the entries of its 8 devices form a permutation of 0 to 31; entry e sends its tile to device e // 4 of that dp index, slot e % 4; the 4 tiles of one device go to 4 different devices, so each device sends at most one tile to each device and receives exactly 4. `seq_lengths`: on each device the tile counts ceil(length / 128) of the 4 slots sum to 4; empty slots occur; every dp index has a device holding one sequence of 512 tokens.
All inputs are finite; a program needn't handle non-finite values.
Results may differ from a plain program's by a relative error of at most 0.014.
The roundings to bfloat16 on the way count: a program that leaves them out, or rounds other values in their place, can miss the bound.
Values may be sent and summed in bfloat16 or wider, within the bound.
No kernel may reach another device: no remote copies, remote signals or barrier semaphores. Data moves between devices by JAX's collectives and lax.ppermute only.
A program may use at most 128 MiB of HBM per device.

v0:
```python
import jax
import jax.numpy as jnp
from jax import lax
from jax.sharding import PartitionSpec as P

HEAD_DIM = 64


SCALE = 0.125
EPSILON = 1e-06
MASKED = -1000000000.0


def normalize(stream, gain, shift):
    middle = jnp.mean(stream, axis=-1, keepdims=True)
    centered = stream - middle
    spread = jnp.mean(centered * centered, axis=-1, keepdims=True)
    return centered * lax.rsqrt(spread + EPSILON) * gain + shift


def gelu_tanh(values):
    return jax.nn.gelu(values, approximate=True)


def layout(lengths, row_count, tile_rows):
    tile_counts = (lengths + tile_rows - 1) // tile_rows
    seg_ends = jnp.cumsum(tile_counts) * tile_rows
    seg_starts = seg_ends - tile_counts * tile_rows
    position = jnp.arange(row_count, dtype=jnp.int32)[:, None]
    inside = (position >= seg_starts[None, :]) & (position < seg_ends[None, :])
    segment = jnp.sum((position >= seg_ends[None, :]).astype(jnp.int32), axis=1)
    offset = jnp.sum(jnp.where(inside, position - seg_starts[None, :], 0), axis=1)
    length_here = jnp.sum(jnp.where(inside, lengths[None, :], 0), axis=1)
    return (segment, offset < length_here)


def across(left, right):
    return lax.dot_general(
        left, right, (((0,), (0,)), ((), ())), preferred_element_type=jnp.float32
    )


def against(left, right):
    return lax.dot_general(
        left, right, (((1,), (1,)), ((), ())), preferred_element_type=jnp.float32
    )


def col_sums(values):
    return jnp.sum(values.astype(jnp.float32), axis=0)


def per_device(
    tokens,
    cotangent,
    tile_dest,
    seq_lengths,
    norm1_gain,
    norm1_bias,
    w_qkv,
    q_bias,
    v_bias,
    w_out,
    out_bias,
    norm2_gain,
    norm2_bias,
    w_up,
    up_bias,
    w_down,
    down_bias,
):
    peer_count = lax.axis_size("fsdp")
    tile_count = tile_dest.shape[0]
    row_count, model_width = tokens.shape
    tile_rows = row_count // tile_count
    flat_width = tile_rows * model_width
    head_count = model_width // HEAD_DIM
    target = tile_dest // tile_count
    slot_index = tile_dest % tile_count
    peer_ids = jnp.arange(peer_count, dtype=jnp.int32)
    sending = target[None, :] == peer_ids[:, None]
    send_table = sending.astype(jnp.bfloat16)
    empty_slot = tile_count * (1 - jnp.sum(sending.astype(jnp.int32), axis=1))
    bucket_slot = jnp.sum(jnp.where(sending, slot_index[None, :], 0), axis=1) + empty_slot
    bucket_tokens = jnp.dot(
        send_table, tokens.reshape(tile_count, flat_width), preferred_element_type=jnp.float32
    ).astype(jnp.bfloat16)
    bucket_cot = jnp.dot(
        send_table, cotangent.reshape(tile_count, flat_width), preferred_element_type=jnp.float32
    ).astype(jnp.bfloat16)
    got_tokens, got_cot, got_slot = (
        lax.all_to_all(bucket_tokens, "fsdp", split_axis=0, concat_axis=0, tiled=True),
        lax.all_to_all(bucket_cot, "fsdp", split_axis=0, concat_axis=0, tiled=True),
        lax.all_to_all(bucket_slot, "fsdp", split_axis=0, concat_axis=0, tiled=True),
    )
    placing = got_slot[None, :] == jnp.arange(tile_count, dtype=jnp.int32)[:, None]
    place_table = placing.astype(jnp.bfloat16)
    local_tokens = (
        jnp.dot(place_table, got_tokens, preferred_element_type=jnp.float32)
        .astype(jnp.bfloat16)
        .reshape(row_count, model_width)
    )
    local_cot = (
        jnp.dot(place_table, got_cot, preferred_element_type=jnp.float32)
        .astype(jnp.bfloat16)
        .reshape(row_count, model_width)
    )

    def to_buckets(local_rows):
        return across(place_table, local_rows.reshape(tile_count, flat_width)).astype(jnp.bfloat16)

    def from_buckets(got_rows):
        return across(send_table, got_rows).astype(jnp.bfloat16).reshape(row_count, model_width)

    (
        gain_one,
        shift_one,
        mat_qkv,
        bias_q,
        bias_v,
        mat_out,
        bias_out,
        gain_two,
        shift_two,
        mat_up,
        bias_up,
        mat_down,
        bias_down,
    ) = (
        lax.all_gather(norm1_gain.astype(jnp.bfloat16), ("dp", "fsdp"), axis=0, tiled=True),
        lax.all_gather(norm1_bias.astype(jnp.bfloat16), ("dp", "fsdp"), axis=0, tiled=True),
        lax.all_gather(w_qkv.astype(jnp.bfloat16), ("dp", "fsdp"), axis=0, tiled=True),
        lax.all_gather(q_bias.astype(jnp.bfloat16), ("dp", "fsdp"), axis=0, tiled=True),
        lax.all_gather(v_bias.astype(jnp.bfloat16), ("dp", "fsdp"), axis=0, tiled=True),
        lax.all_gather(w_out.astype(jnp.bfloat16), ("dp", "fsdp"), axis=0, tiled=True),
        lax.all_gather(out_bias.astype(jnp.bfloat16), ("dp", "fsdp"), axis=0, tiled=True),
        lax.all_gather(norm2_gain.astype(jnp.bfloat16), ("dp", "fsdp"), axis=0, tiled=True),
        lax.all_gather(norm2_bias.astype(jnp.bfloat16), ("dp", "fsdp"), axis=0, tiled=True),
        lax.all_gather(w_up.astype(jnp.bfloat16), ("dp", "fsdp"), axis=0, tiled=True),
        lax.all_gather(up_bias.astype(jnp.bfloat16), ("dp", "fsdp"), axis=0, tiled=True),
        lax.all_gather(w_down.astype(jnp.bfloat16), ("dp", "fsdp"), axis=0, tiled=True),
        lax.all_gather(down_bias.astype(jnp.bfloat16), ("dp", "fsdp"), axis=0, tiled=True),
    )
    gain_one_f = gain_one.astype(jnp.float32)
    shift_one_f = shift_one.astype(jnp.float32)
    gain_two_f = gain_two.astype(jnp.float32)
    shift_two_f = shift_two.astype(jnp.float32)
    segment, valid_rows = layout(seq_lengths[0], row_count, tile_rows)
    allowed_pairs = (segment[:, None] == segment[None, :]) & valid_rows[None, :]
    stream = local_tokens.astype(jnp.float32)
    norm_value, norm_one_pull = jax.vjp(normalize, stream, gain_one_f, shift_one_f)
    norm_one = norm_value.astype(jnp.bfloat16)
    qkv_shift = jnp.concatenate(
        [
            bias_q.astype(jnp.float32),
            jnp.zeros((model_width,), jnp.float32),
            bias_v.astype(jnp.float32),
        ]
    )
    qkv_low = (jnp.dot(norm_one, mat_qkv, preferred_element_type=jnp.float32) + qkv_shift).astype(
        jnp.bfloat16
    )
    queries = qkv_low[:, :model_width]
    key_rows = qkv_low[:, model_width : 2 * model_width]
    values = qkv_low[:, 2 * model_width :]

    def head_forward(head_index, loop_state):
        merged, lse_rows = loop_state
        col_start = head_index * HEAD_DIM
        query_head = lax.dynamic_slice_in_dim(queries, col_start, HEAD_DIM, 1)
        key_head = lax.dynamic_slice_in_dim(key_rows, col_start, HEAD_DIM, 1)
        value_head = lax.dynamic_slice_in_dim(values, col_start, HEAD_DIM, 1)
        scores = against(query_head, key_head) * SCALE
        scores = jnp.where(allowed_pairs, scores, MASKED)
        row_top = jnp.max(scores, axis=1, keepdims=True)
        exp_scores = jnp.exp(scores - row_top)
        row_total = jnp.sum(exp_scores, axis=1, keepdims=True)
        attn_probs = (exp_scores / row_total).astype(jnp.bfloat16)
        head_out = jnp.dot(attn_probs, value_head, preferred_element_type=jnp.float32)
        merged = lax.dynamic_update_slice_in_dim(merged, head_out, col_start, 1)
        lse_rows = lax.dynamic_update_slice_in_dim(
            lse_rows, (row_top + jnp.log(row_total)).reshape(1, row_count), head_index, 0
        )
        return (merged, lse_rows)

    merged, lse_rows = lax.fori_loop(
        0,
        head_count,
        head_forward,
        (
            jnp.zeros((row_count, model_width), jnp.float32),
            jnp.zeros((head_count, row_count), jnp.float32),
        ),
    )
    attn_out = merged.astype(jnp.bfloat16)
    mid_stream = (
        stream
        + jnp.dot(attn_out, mat_out, preferred_element_type=jnp.float32)
        + bias_out.astype(jnp.float32)
    )
    norm_value_two, norm_two_pull = jax.vjp(normalize, mid_stream, gain_two_f, shift_two_f)
    norm_two = norm_value_two.astype(jnp.bfloat16)
    pre_act = jnp.dot(norm_two, mat_up, preferred_element_type=jnp.float32) + bias_up.astype(
        jnp.float32
    )
    act_value, gelu_pull = jax.vjp(gelu_tanh, pre_act)
    act_low = act_value.astype(jnp.bfloat16)
    result = (
        mid_stream
        + jnp.dot(act_low, mat_down, preferred_element_type=jnp.float32)
        + bias_down.astype(jnp.float32)
    )
    back_result = lax.all_to_all(
        to_buckets(result.astype(jnp.bfloat16)), "fsdp", split_axis=0, concat_axis=0, tiled=True
    )
    mixed = from_buckets(back_result)
    gain_one, mat_qkv, mat_out, gain_two, mat_up, mat_down = (
        lax.all_gather(norm1_gain.astype(jnp.bfloat16), ("dp", "fsdp"), axis=0, tiled=True),
        lax.all_gather(w_qkv.astype(jnp.bfloat16), ("dp", "fsdp"), axis=0, tiled=True),
        lax.all_gather(w_out.astype(jnp.bfloat16), ("dp", "fsdp"), axis=0, tiled=True),
        lax.all_gather(norm2_gain.astype(jnp.bfloat16), ("dp", "fsdp"), axis=0, tiled=True),
        lax.all_gather(w_up.astype(jnp.bfloat16), ("dp", "fsdp"), axis=0, tiled=True),
        lax.all_gather(w_down.astype(jnp.bfloat16), ("dp", "fsdp"), axis=0, tiled=True),
    )
    gain_one_f = gain_one.astype(jnp.float32)
    gain_two_f = gain_two.astype(jnp.float32)
    norm_value, norm_one_pull = jax.vjp(normalize, stream, gain_one_f, shift_one_f)
    norm_value_two, norm_two_pull = jax.vjp(normalize, mid_stream, gain_two_f, shift_two_f)
    grad_out_rows = local_cot.astype(jnp.float32) * valid_rows.astype(jnp.float32)[:, None]
    grad_out_low = grad_out_rows.astype(jnp.bfloat16)
    d_down_bias = col_sums(grad_out_low)
    d_w_down = across(act_low, grad_out_low)
    d_act = against(grad_out_low, mat_down)
    d_pre = gelu_pull(d_act)[0].astype(jnp.bfloat16)
    d_up_bias = col_sums(d_pre)
    d_w_up = across(norm_two, d_pre)
    d_norm_two = against(d_pre, mat_up)
    d_mid_norm, d_gain_two, d_shift_two = norm_two_pull(d_norm_two)
    d_mid = grad_out_rows + d_mid_norm
    d_proj_low = d_mid.astype(jnp.bfloat16)
    d_out_bias = col_sums(d_proj_low)
    d_w_out = across(attn_out, d_proj_low)
    d_attn = against(d_proj_low, mat_out).astype(jnp.bfloat16)

    def head_backward(head_index, grad_buf):
        col_start = head_index * HEAD_DIM
        query_head = lax.dynamic_slice_in_dim(queries, col_start, HEAD_DIM, 1)
        key_head = lax.dynamic_slice_in_dim(key_rows, col_start, HEAD_DIM, 1)
        value_head = lax.dynamic_slice_in_dim(values, col_start, HEAD_DIM, 1)
        d_head = lax.dynamic_slice_in_dim(d_attn, col_start, HEAD_DIM, 1)
        lse_head = lax.dynamic_slice_in_dim(lse_rows, head_index, 1, 0).reshape(row_count, 1)
        scores = against(query_head, key_head) * SCALE
        attn_probs = jnp.where(allowed_pairs, jnp.exp(scores - lse_head), 0.0)
        probs_low = attn_probs.astype(jnp.bfloat16)
        d_value = across(probs_low, d_head)
        d_probs = against(d_head, value_head)
        d_scores = attn_probs * (d_probs - jnp.sum(attn_probs * d_probs, axis=1, keepdims=True))
        scores_low = d_scores.astype(jnp.bfloat16)
        d_query = jnp.dot(scores_low, key_head, preferred_element_type=jnp.float32) * SCALE
        d_key = across(scores_low, query_head) * SCALE
        grad_buf = lax.dynamic_update_slice_in_dim(grad_buf, d_query, col_start, 1)
        grad_buf = lax.dynamic_update_slice_in_dim(grad_buf, d_key, model_width + col_start, 1)
        grad_buf = lax.dynamic_update_slice_in_dim(
            grad_buf, d_value, 2 * model_width + col_start, 1
        )
        return grad_buf

    grad_buf = lax.fori_loop(
        0, head_count, head_backward, jnp.zeros((row_count, 3 * model_width), jnp.float32)
    )
    d_qkv = grad_buf.astype(jnp.bfloat16)
    d_q_bias = col_sums(d_qkv[:, :model_width])
    d_v_bias = col_sums(d_qkv[:, 2 * model_width :])
    d_w_qkv = across(norm_one, d_qkv)
    d_norm_one = against(d_qkv, mat_qkv)
    d_in_norm, d_gain_one, d_shift_one = norm_one_pull(d_norm_one)
    d_stream = d_mid + d_in_norm
    back_grad = lax.all_to_all(
        to_buckets(d_stream.astype(jnp.bfloat16)), "fsdp", split_axis=0, concat_axis=0, tiled=True
    )
    grad_tokens = from_buckets(back_grad)
    (
        s_gain_one,
        s_shift_one,
        s_w_qkv,
        s_q_bias,
        s_v_bias,
        s_w_out,
        s_out_bias,
        s_gain_two,
        s_shift_two,
        s_w_up,
        s_up_bias,
        s_w_down,
        s_down_bias,
    ) = (
        lax.psum_scatter(d_gain_one, ("dp", "fsdp"), scatter_dimension=0, tiled=True),
        lax.psum_scatter(d_shift_one, ("dp", "fsdp"), scatter_dimension=0, tiled=True),
        lax.psum_scatter(d_w_qkv, ("dp", "fsdp"), scatter_dimension=0, tiled=True),
        lax.psum_scatter(d_q_bias, ("dp", "fsdp"), scatter_dimension=0, tiled=True),
        lax.psum_scatter(d_v_bias, ("dp", "fsdp"), scatter_dimension=0, tiled=True),
        lax.psum_scatter(d_w_out, ("dp", "fsdp"), scatter_dimension=0, tiled=True),
        lax.psum_scatter(d_out_bias, ("dp", "fsdp"), scatter_dimension=0, tiled=True),
        lax.psum_scatter(d_gain_two, ("dp", "fsdp"), scatter_dimension=0, tiled=True),
        lax.psum_scatter(d_shift_two, ("dp", "fsdp"), scatter_dimension=0, tiled=True),
        lax.psum_scatter(d_w_up, ("dp", "fsdp"), scatter_dimension=0, tiled=True),
        lax.psum_scatter(d_up_bias, ("dp", "fsdp"), scatter_dimension=0, tiled=True),
        lax.psum_scatter(d_w_down, ("dp", "fsdp"), scatter_dimension=0, tiled=True),
        lax.psum_scatter(d_down_bias, ("dp", "fsdp"), scatter_dimension=0, tiled=True),
    )
    return (
        mixed,
        grad_tokens,
        s_gain_one,
        s_shift_one,
        s_w_qkv,
        s_q_bias,
        s_v_bias,
        s_w_out,
        s_out_bias,
        s_gain_two,
        s_shift_two,
        s_w_up,
        s_up_bias,
        s_w_down,
        s_down_bias,
    )


def solution(mesh):
    in_specs = (
        P(("dp", "fsdp"), None),
        P(("dp", "fsdp"), None),
        P(("dp", "fsdp")),
        P(("dp", "fsdp"), None),
        P(("dp", "fsdp")),
        P(("dp", "fsdp")),
        P(("dp", "fsdp"), None),
        P(("dp", "fsdp")),
        P(("dp", "fsdp")),
        P(("dp", "fsdp"), None),
        P(("dp", "fsdp")),
        P(("dp", "fsdp")),
        P(("dp", "fsdp")),
        P(("dp", "fsdp"), None),
        P(("dp", "fsdp")),
        P(("dp", "fsdp"), None),
        P(("dp", "fsdp")),
    )
    out_specs = (
        P(("dp", "fsdp"), None),
        P(("dp", "fsdp"), None),
        P(("dp", "fsdp")),
        P(("dp", "fsdp")),
        P(("dp", "fsdp"), None),
        P(("dp", "fsdp")),
        P(("dp", "fsdp")),
        P(("dp", "fsdp"), None),
        P(("dp", "fsdp")),
        P(("dp", "fsdp")),
        P(("dp", "fsdp")),
        P(("dp", "fsdp"), None),
        P(("dp", "fsdp")),
        P(("dp", "fsdp"), None),
        P(("dp", "fsdp")),
    )
    return jax.shard_map(
        per_device, mesh=mesh, in_specs=in_specs, out_specs=out_specs, check_vma=False
    )
```

profile of v0, /device:TPU:0, one launch (start us, length us, event | category | flops | bytes accessed | tf_op | source)
XLA Modules:
  0.0 865.0 jit_solution(973319603198711765)
XLA Ops:
  13.7 7.3 all-to-all-start
  24.7 2.5 reshape.307
  27.4 5.9 all-to-all-start.1
  34.8 1.9 fusion.34
  36.7 2.6 reduce.3
  39.2 3.9 reshape.311
  43.3 40.7 %all-to-all-done.1 = bf16[8,2,49152]{2,1,0:T(2,128)(2,1)S(1)} async-done(((bf16[8,2,49152]{2,1,0:T(2,128)(2,1)}), bf16[8,2,49152]{2,1,0:T(2,128)(2,1)S(1)}, u32[]{:S(2)}, u32[]{:S(2)}) %all-to-all-start.1) | async-done | bytes 1572896 | tf_op jit(solution)/shard_map/all_to_all | solution.py:92
  85.1 4.3 all-to-all-start.3
  92.4 55.5 %all-reduce.19 = (bf16[768]{0:T(1024)(128)(2,1)S(1)}, bf16[768]{0:T(1024)(128)(2,1)S(1)}, bf16[768]{0:T(1024)(128)(2,1)S(1)}, bf16[768]{0:T(1024)(128)(2,1)S(1)}...) all-reduce(bf16[768]{0:T(1024)(128)(2,1)S(1)} %dynamic-update-slice, ...), channel_id=1, replica_groups=mesh['dp'=4,'fsdp'=8] {'dp','fsdp'}, use_global_device_ids=true, to_apply=%add.4 | all-reduce | flops 9216 | bytes 36864
  148.5 4.7 reshape.308
  153.2 3.0 fusion.36
  156.2 2.5 reshape.286
  159.2 6.4 reshape.312
  165.6 5.0 fusion.37
  170.6 2.5 reshape.287
  174.3 4.1 fusion.45
  180.0 36.1 %while.32 = (s32[]{:T(128)}, bf16[512,768]{0,1:T(8,128)(2,1)S(1)}, f32[12,512]{1,0:T(8,128)S(1)}, bf16[512,768]{1,0:T(8,128)(2,1)}, bf16[512,768]{1,0:T(8,128)(2...) while((s32[]{:T(128)}, bf16[512,768]{0,1:T(8,128)(2,1)S(1)}, ...), condition=%wide.region_11.12_spmd.clone, body=%wide.region_8.11_spmd.clone.sunk | while | flops 69729792 | bytes 3697327 | solution.py:186
  217.1 2.5 fusion.81
  219.9 7.2 fusion.73
  227.2 56.7 %all-gather.11.cloned.1.call-done = bf16[3072,768]{1,0:T(8,128)(2,1)} async-done(((bf16[96,768]{1,0:T(8,128)(2,1)}), bf16[3072,768]{1,0:T(8,128)(2,1)}) %all-gather.11.cloned.1.call-update) | async-done | bytes 4718608 | tf_op jit(solution)/shard_map/all_gather | solution.py:141
  283.9 9.2 %convert_reduce_fusion = (f32[3072]{0:T(1024)S(1)}, bf16[512,3072]{1,0:T(8,128)(2,1)S(1)}) fusion(f32[512,3072]{1,0:T(8,128)} %fusion.73, f32[3072]{0:T(1024)S(1)} %convert_element_type.231, bf16[512,768]{1,0:T(8,128)(2,1)} %get-tuple-element.450, bf16[3072,768]{1,0:T(8,128)(2,1)} %all-gather.11.cloned.1.call-done), kind=kOutput, calls=%fused_computation.65 | convolution fusion | flops 2452091904 | bytes 14966784 | tf_op jit(solution)/shard_map/dot_general | solution.py:44
  293.2 3.0 multiply_reduce_fusion.1
  298.7 2.2 fusion.54
  301.0 3.1 convolution_convert_fusion.8
  305.7 106.2 %while.33 = (s32[]{:T(128)}, bf16[512,2304]{0,1:T(8,128)(2,1)}, bf16[512,768]{1,0:T(8,128)(2,1)}, bf16[512,768]{1,0:T(8,128)(2,1)}, f32[12,512]{1,0:T(8,128)S(1)...) while((s32[]{:T(128)}, bf16[512,2304]{0,1:T(8,128)(2,1)}, ...), condition=%wide.region_18.19_spmd.clone, body=%wide.region_16.18_spmd.clone.sunk | while | flops 170720768 | bytes 9192280 | solution.py:268
  310.8 1.9 fusion.131
  319.6 1.9 fusion.131
  321.5 1.9 convolution_dynamic-update-slice_fusion.5
  328.5 1.9 fusion.131
  337.3 1.9 fusion.131
  346.1 1.9 fusion.131
  355.0 1.9 fusion.131
  356.9 1.9 convolution_dynamic-update-slice_fusion.5
  363.8 1.9 fusion.131
  365.7 1.9 convolution_dynamic-update-slice_fusion.5
  372.7 1.9 fusion.131
  374.6 1.9 convolution_dynamic-update-slice_fusion.5
  383.4 1.9 convolution_dynamic-update-slice_fusion.5
  390.4 1.9 fusion.131
  392.3 1.9 convolution_dynamic-update-slice_fusion.5
  399.2 1.9 fusion.131
  408.1 1.9 fusion.131
  411.8 6.8 fusion.71
  420.1 7.2 fusion.72
  427.6 10.7 %fusion.74 = f32[3072,768]{1,0:T(8,128)} fusion(bf16[512,768]{1,0:T(8,128)(2,1)} %get-tuple-element.450, f32[512,3072]{1,0:T(8,128)} %fusion.73, f32[3072]{0:T(1024)S(1)} %convert_element_type.231), kind=kOutput, calls=%fused_computation.153 | convolution fusion | flops 2431647744 | bytes 16527360 | tf_op jit(solution)/shard_map/dot_general | solution.py:38
  438.3 9.4 %add_convert_fusion.1 = bf16[512,768]{1,0:T(8,128)(2,1)} fusion(f32[512,768]{1,0:T(8,128)S(1)} %copy-done.5, bf16[3072,768]{1,0:T(8,128)(2,1)} %all-gather.11.cloned.1.call-done, f32[768]{0:T(1024)S(1)} %convert_element_type.235, f32[512,3072]{1,0:T(8,128)} %fusion.73, f32[3072]{0:T(1024)S(1)} %convert_element_type.231), kind=kOutput, calls=%fused_computation.89 | convolution fusion | flops 2432827392 | bytes 13384704 | tf_op jit(solution)/shard_map/dot_general | solution.py:210
  447.6 2.6 reshape.281
  452.1 2.5 reduce.2
  454.6 4.0 reshape.309
  458.6 4.2 all-to-all-start.2
  462.8 5.2 multiply_reduce_fusion.2
  473.3 2.6 reduce.4
  475.9 3.9 reshape.313
  479.8 39.3 %all-to-all-done.2 = bf16[8,2,49152]{2,1,0:T(2,128)(2,1)S(1)} async-done(((bf16[8,2,49152]{2,1,0:T(2,128)(2,1)}), bf16[8,2,49152]{2,1,0:T(2,128)(2,1)S(1)}, u32[]{:S(2)}, u32[]{:S(2)}) %all-to-all-start.2) | async-done | bytes 1572896 | tf_op jit(solution)/shard_map/all_to_all | solution.py:213
  520.4 4.3 all-to-all-start.4
  526.4 65.7 %all-reduce.18 = (f32[768]{0:T(1024)S(1)}, f32[768]{0:T(1024)S(1)}, f32[768]{0:T(1024)S(1)}, f32[768]{0:T(1024)S(1)}, f32[768]{0:T(1024)S(1)}, /*index=5*/f32[76...) all-reduce(f32[768]{0:T(1024)S(1)} %get-tuple-element.386, ...), channel_id=2, replica_groups=mesh['dp'=4,'fsdp'=8] {'dp','fsdp'}, use_global_device_ids=true, to_apply=%region_22.23.clone | all-reduce | flops 9216 | bytes 73728
  597.4 4.8 reshape.310
  602.2 2.8 convolution_convert_fusion.6
  604.9 2.7 reshape.282
  607.7 4.7 reshape.314
  612.4 2.8 convolution_convert_fusion.4
  615.2 2.7 reshape.285
  617.9 98.1 %reduce-scatter.9.cloned.1.call-done = f32[24,3072]{1,0:T(8,128)} async-done(((f32[768,3072]{1,0:T(8,128)}), f32[24,3072]{1,0:T(8,128)}) %reduce-scatter.9.cloned.1.call-update) | async-done | bytes 294928 | tf_op jit(solution)/shard_map/reduce_scatter | solution.py:306
  716.1 141.9 %reduce-scatter.11.cloned.1.call-done = f32[96,768]{1,0:T(8,128)} async-done(((f32[3072,768]{1,0:T(8,128)}), f32[96,768]{1,0:T(8,128)}) %reduce-scatter.11.cloned.1.call-update) | async-done | bytes 294928 | tf_op jit(solution)/shard_map/reduce_scatter | solution.py:308
  (292 shorter events, 151.2 us)
Async XLA Ops:
  7.2 13.8 %copy-start.10 = (bf16[512,768]{1,0:T(8,128)(2,1)S(1)}, bf16[512,768]{1,0:T(8,128)(2,1)}, u32[]{:S(2)}) copy-start(bf16[512,768]{1,0:T(8,128)(2,1)} %param.21) | copy-start | bytes 2359300
  7.2 167.1 %all-gather.5.cloned.1.call-start = ((), (), s32[]{:S(2)}) async-start(), calls=%async_computation.9 | async-start | bytes 3649536 | tf_op jit(solution)/shard_map/all_gather | solution.py:132
  8.9 207.3 %all-gather.7.cloned.1.call-start = ((), (), s32[]{:S(2)}) async-start(), calls=%async_computation.10 | async-start | bytes 1216512 | tf_op jit(solution)/shard_map/all_gather | solution.py:135
  10.5 209.4 %all-gather.9.cloned.1.call-start = ((), (), s32[]{:S(2)}) async-start(), calls=%async_computation.11 | async-start | bytes 4866048 | tf_op jit(solution)/shard_map/all_gather | solution.py:139
  13.7 13.7 %all-to-all-start = ((s32[8,1,1]{2,1,0:T(1,128)}), s32[8,1,1]{2,1,0:T(1,128)S(1)}, u32[]{:S(2)}, u32[]{:S(2)}) async-start(s32[8,1,1]{2,1,0:T(1,128)} %copy.42), calls=%async_computation | async-start | bytes 8192 | tf_op jit(solution)/shard_map/all_to_all | solution.py:94
  27.2 6.1 copy-start.11
  27.4 56.6 %all-to-all-start.1 = ((bf16[8,2,49152]{2,1,0:T(2,128)(2,1)}), bf16[8,2,49152]{2,1,0:T(2,128)(2,1)S(1)}, u32[]{:S(2)}, u32[]{:S(2)}) async-start(bf16[8,2,49152]{2,1,0:T(2,128)(2,1)} %reshape.307), calls=%async_computation.1 | async-start | bytes 3145728 | tf_op jit(solution)/shard_map/all_to_all | solution.py:92
  43.2 46.3 %copy-start.12 = (f32[96,768]{1,0:T(8,128)S(1)}, f32[96,768]{1,0:T(8,128)}, u32[]{:S(2)}) copy-start(f32[96,768]{1,0:T(8,128)} %param.36) | copy-start | bytes 884740
  43.2 47.1 %copy-start.15 = (f32[24]{0:T(128)S(1)}, f32[24]{0:T(128)}, u32[]{:S(2)}) copy-start(f32[24]{0:T(128)} %param.31) | copy-start | bytes 292
  43.2 47.1 %copy-start.16 = (f32[24]{0:T(128)S(1)}, f32[24]{0:T(128)}, u32[]{:S(2)}) copy-start(f32[24]{0:T(128)} %param.29) | copy-start | bytes 292
  43.2 47.1 %copy-start.17 = (f32[24]{0:T(128)S(1)}, f32[24]{0:T(128)}, u32[]{:S(2)}) copy-start(f32[24]{0:T(128)} %param.28) | copy-start | bytes 292
  43.2 47.1 %copy-start.18 = (f32[24]{0:T(128)S(1)}, f32[24]{0:T(128)}, u32[]{:S(2)}) copy-start(f32[24]{0:T(128)} %param.26) | copy-start | bytes 292
  43.2 47.1 %copy-start.19 = (f32[24]{0:T(128)S(1)}, f32[24]{0:T(128)}, u32[]{:S(2)}) copy-start(f32[24]{0:T(128)} %param.25) | copy-start | bytes 292
  43.2 47.2 %copy-start.20 = (f32[24]{0:T(128)S(1)}, f32[24]{0:T(128)}, u32[]{:S(2)}) copy-start(f32[24]{0:T(128)} %param.37) | copy-start | bytes 292
  43.2 47.2 %copy-start.21 = (f32[24]{0:T(128)S(1)}, f32[24]{0:T(128)}, u32[]{:S(2)}) copy-start(f32[24]{0:T(128)} %param.33) | copy-start | bytes 292
  43.2 47.2 %copy-start.22 = (f32[24]{0:T(128)S(1)}, f32[24]{0:T(128)}, u32[]{:S(2)}) copy-start(f32[24]{0:T(128)} %param.32) | copy-start | bytes 292
  43.2 47.2 %copy-start.23 = (f32[96]{0:T(128)S(1)}, f32[96]{0:T(128)}, u32[]{:S(2)}) copy-start(f32[96]{0:T(128)} %param.35) | copy-start | bytes 1156
  43.3 104.6 %copy-start.13 = (s32[1,4]{1,0:T(1,128)S(1)}, s32[1,4]{1,0:T(1,128)}, u32[]{:S(2)}) copy-start(s32[1,4]{1,0:T(1,128)} %param.24) | copy-start | bytes 52
  84.0 1.1 copy-start.6
  85.1 74.1 %all-to-all-start.3 = ((bf16[8,2,49152]{2,1,0:T(2,128)(2,1)}), bf16[8,2,49152]{2,1,0:T(2,128)(2,1)}, u32[]{:S(2)}, u32[]{:S(2)}) async-start(bf16[8,2,49152]{2,1,0:T(2,128)(2,1)} %reshape.311), calls=%async_computation.3 | async-start | bytes 3145728 | tf_op jit(solution)/shard_map/all_to_all | solution.py:93
  89.4 194.5 %all-gather.11.cloned.1.call-start = ((), (), s32[]{:S(2)}) async-start(), calls=%async_computation.12 | async-start | bytes 4866048 | tf_op jit(solution)/shard_map/all_gather | solution.py:141
  90.2 527.7 %reduce-scatter.7.cloned.1.call-start = ((), (), s32[]{:S(2)}) async-start(), calls=%async_computation.14 | async-start | bytes 2433024 | tf_op jit(solution)/shard_map/reduce_scatter | solution.py:302
  173.1 5.4 copy-start.2
  216.1 1.0 copy-start.8
  219.6 76.6 %copy-start.4 = (f32[512,768]{1,0:T(8,128)}, f32[512,768]{1,0:T(8,128)S(1)}, u32[]{:S(2)}) copy-start(f32[512,768]{1,0:T(8,128)S(1)} %get-tuple-element.471) | copy-start | bytes 4718596
  283.9 9.2 %copy-start.14 = (bf16[768,3072]{1,0:T(8,128)(2,1)S(1)}, bf16[768,3072]{1,0:T(8,128)(2,1)}, u32[]{:S(2)}) copy-start(bf16[768,3072]{1,0:T(8,128)(2,1)} %all-gather.9.cloned.1.call-done) | copy-start | bytes 14155780
  293.1 3.0 copy-start.24
  296.2 1.4 copy-start.3
  297.6 1.1 copy-start.9
  297.9 3.1 copy-start
  301.0 316.9 %reduce-scatter.5.cloned.1.call-start = ((), (), s32[]{:S(2)}) async-start(), calls=%async_computation.13 | async-start | bytes 7299072 | tf_op jit(solution)/shard_map/reduce_scatter | solution.py:299
  418.7 1.4 copy-start.5
  418.7 297.4 %reduce-scatter.9.cloned.1.call-start = ((), (), s32[]{:S(2)}) async-start(), calls=%async_computation.15 | async-start | bytes 9732096 | tf_op jit(solution)/shard_map/reduce_scatter | solution.py:306
  427.3 430.7 %reduce-scatter.11.cloned.1.call-start = ((), (), s32[]{:S(2)}) async-start(), calls=%async_computation.16 | async-start | bytes 9732096 | tf_op jit(solution)/shard_map/reduce_scatter | solution.py:308
  458.6 60.6 %all-to-all-start.2 = ((bf16[8,2,49152]{2,1,0:T(2,128)(2,1)}), bf16[8,2,49152]{2,1,0:T(2,128)(2,1)S(1)}, u32[]{:S(2)}, u32[]{:S(2)}) async-start(bf16[8,2,49152]{2,1,0:T(2,128)(2,1)} %reshape.309), calls=%async_computation.2 | async-start | bytes 3145728 | tf_op jit(solution)/shard_map/all_to_all | solution.py:213
  468.0 1.9 copy-start.1
  519.2 1.2 copy-start.7
  520.4 87.3 %all-to-all-start.4 = ((bf16[8,2,49152]{2,1,0:T(2,128)(2,1)}), bf16[8,2,49152]{2,1,0:T(2,128)(2,1)}, u32[]{:S(2)}, u32[]{:S(2)}) async-start(bf16[8,2,49152]{2,1,0:T(2,128)(2,1)} %reshape.313), calls=%async_computation.4 | async-start | bytes 3145728 | tf_op jit(solution)/shard_map/all_to_all | solution.py:278
Sparse Core Ops, SparseCore 0:
  11.5 75.0 all-gather.4
  90.1 62.5 all-gather.6
  156.2 62.4 all-gather.8
  222.0 61.8 all-gather.10
  301.1 97.9 reduce-scatter.6
  418.8 156.4 reduce-scatter.4
  581.8 134.2 reduce-scatter.8
  722.5 135.4 reduce-scatter.10
where the time goes:
time: 876 us; the launch traced here: 865 us
  waiting for transfers between devices  377 us (43%)
  matrix products  225 us (26%)
  blocking collectives  121 us (14%)
  local copies, waits for them, and re-layouts  71.4 us (8%)
  other arithmetic  27.3 us (3%)
  starting transfers between devices  26.6 us (3%)
  between operations  15 us (2%)
    reduce_scatter x1, waiting for transfers between devices, per_device(): lax.psum_scatter(d_w_down, ('dp', 'fsdp'), scatter_dimension=0, tiled=True)  142 us
    unnamed x2, blocking collectives  121 us
    reduce_scatter x1, waiting for transfers between devices, per_device(): lax.psum_scatter(d_w_up, ('dp', 'fsdp'), scatter_dimension=0, tiled=True)  98.1 us
    dot_general x32, matrix products, across(): lax.dot_general(left, right, (((0,), (0,)), ((), ())), preferred_element_...  81.3 us
    dot_general x40, matrix products, against(): lax.dot_general(left, right, (((1,), (1,)), ((), ())), preferred_element_...  73.1 us
    all_gather x1, waiting for transfers between devices, per_device(): lax.all_gather(w_down.astype(jnp.bfloat16), ('dp', 'fsdp'), axis=0, tiled...  56.7 us
    unnamed x85, local copies, waits for them, and re-layouts  49.6 us
    all_to_all x1, waiting for transfers between devices, per_device(): lax.all_to_all(bucket_tokens, 'fsdp', split_axis=0, concat_axis=0, tiled=...  40.7 us
  transfers between devices with their start and end apart: 13, of which 6 were waited for; matrix products, arithmetic and copies ran while one was open for 35% of the time, Pallas kernels for 0%

commit v1 on v0

v1 whole, which is shorter than its diff:
```python
import functools

import jax
import jax.numpy as jnp
from jax import lax
from jax.experimental import pallas as pl
from jax.experimental.pallas import tpu as pltpu
from jax.sharding import PartitionSpec as P

HEAD_DIM = 64
LANES = 128
SCALE = 0.125
EPSILON = 1e-06
MASKED = -1000000000.0
F32 = jnp.float32
BF16 = jnp.bfloat16
AXES = ("dp", "fsdp")


def bits_of(size):
    return size.bit_length() - 1


class Cube:
    def __init__(self, dp_size, fs_size):
        self.size = {"dp": dp_size, "fsdp": fs_size}
        high_dp = [("dp", b) for b in range(1, bits_of(dp_size))]
        high_fs = [("fsdp", b) for b in range(1, bits_of(fs_size))]
        low_fs = [("fsdp", 0)]
        self.core = ("dp", 0)
        self.orders = (high_fs + high_dp + low_fs, high_fs + low_fs + high_dp)
        self.shared = len(high_fs)
        self.natural = [("dp", b) for b in reversed(range(bits_of(dp_size)))] + [
            ("fsdp", b) for b in reversed(range(bits_of(fs_size)))
        ]

    def swap(self, value, link):
        axis, bit = link
        pairs = [(i, i ^ (1 << bit)) for i in range(self.size[axis])]
        return lax.ppermute(value, axis, pairs)

    def my_bit(self, link):
        axis, bit = link
        return (lax.axis_index(axis) >> bit) & 1


def gather_parts(cube, shard, cut):
    held = shard[None]
    for link in cube.orders[0][: cube.shared]:
        held = jnp.concatenate([held, cube.swap(held, link)], axis=0)
    dim, at = cut
    parts = [
        lax.slice_in_dim(held, 0, at, axis=dim + 1),
        lax.slice_in_dim(held, at, shard.shape[dim], axis=dim + 1),
    ]
    for step in range(cube.shared, len(cube.orders[0])):
        moved = [cube.swap(parts[i], cube.orders[i][step]) for i in range(2)]
        parts = [jnp.concatenate([parts[i], moved[i]], axis=0) for i in range(2)]
    others = [cube.swap(part, cube.core) for part in parts]
    return [(parts[0], others[0]), (parts[1], others[1])]


def assemble(cube, halves, me, shapes, plan):
    dp_high = cube.size["dp"] // 2
    fs_size = cube.size["fsdp"]

    def slot(order, a, f):
        where = 0
        for k, (axis, bit) in enumerate(order):
            value = (a >> (bit - 1)) & 1 if axis == "dp" else (f >> bit) & 1
            where = where + (value << k)
        return where

    def kernel(me_ref, own_p, other_p, own_q, other_q, *out_refs):
        core = me_ref[0] & 1
        for out_ref, pieces in zip(out_refs, plan):
            for part, source, target in pieces:
                own, other = ((own_p, other_p), (own_q, other_q))[part]
                out_ref[(0, core, 0) + target] = own[(0,) + source]
                out_ref[(0, 1 - core, 0) + target] = other[(0,) + source]

    def spec(part):
        rows, width = halves[part][0].shape[1:]
        order = cube.orders[part]
        return pl.BlockSpec(
            (1, rows, width),
            lambda a, f, me_ref: (slot(order, a ^ (me_ref[0] >> 1), f ^ me_ref[1]), 0, 0),
        )

    outs = pl.pallas_call(
        kernel,
        out_shape=[
            jax.ShapeDtypeStruct((dp_high, 2, fs_size) + shape, BF16) for shape in shapes
        ],
        grid_spec=pltpu.PrefetchScalarGridSpec(
            num_scalar_prefetch=1,
            grid=(dp_high, fs_size),
            in_specs=[spec(0), spec(0), spec(1), spec(1)],
            out_specs=[
                pl.BlockSpec((1, 2, 1) + shape, lambda a, f, me_ref: (a, 0, f, 0, 0))
                for shape in shapes
            ],
        ),
        name="assemble",
    )(me, *halves[0], *halves[1])
    count = dp_high * 2 * fs_size
    return [out.reshape(count * shape[0], shape[1]) for out, shape in zip(outs, shapes)]


def scatter_sum(cube, parts, rows):
    state = []
    for i, part in enumerate(parts):
        bits = list(cube.natural)
        state.append((part.reshape((2,) * len(bits) + (rows[i], part.shape[1])), bits))
    links = [[cube.core] + list(reversed(order)) for order in cube.orders]
    for step in range(len(links[0])):
        last = step == len(links[0]) - 1
        new_state = []
        for i in range(2):
            value, bits = state[i]
            link = links[i][step]
            dim = bits.index(link)
            mine = cube.my_bit(link)
            give = lax.dynamic_index_in_dim(value, 1 - mine, dim, keepdims=False)
            keep = lax.dynamic_index_in_dim(value, mine, dim, keepdims=False)
            got = cube.swap(give, link)
            total = keep.astype(F32) + got.astype(F32)
            new_state.append(
                (total if last else total.astype(BF16), bits[:dim] + bits[dim + 1 :])
            )
        state = new_state
    return [value for value, _ in state]


def pick_tiles(arrays, index, count):
    def kernel(index_ref, *refs):
        half = len(refs) // 2
        for k in range(half):
            refs[half + k][...] = refs[k][...]

    shape = arrays[0].shape[1:]
    return pl.pallas_call(
        kernel,
        out_shape=[jax.ShapeDtypeStruct((count,) + shape, a.dtype) for a in arrays],
        grid_spec=pltpu.PrefetchScalarGridSpec(
            num_scalar_prefetch=1,
            grid=(count,),
            in_specs=[
                pl.BlockSpec((1,) + shape, lambda i, index_ref: (index_ref[i], 0, 0))
                for _ in arrays
            ],
            out_specs=[
                pl.BlockSpec((1,) + shape, lambda i, index_ref: (i, 0, 0)) for _ in arrays
            ],
        ),
        name="pick_tiles",
    )(index, *arrays)


def dot_nn(left, right):
    return jnp.dot(left, right, preferred_element_type=F32)


def dot_tn(left, right):
    return lax.dot_general(left, right, (((0,), (0,)), ((), ())), preferred_element_type=F32)


def dot_nt(left, right):
    return lax.dot_general(left, right, (((1,), (1,)), ((), ())), preferred_element_type=F32)


def attend_forward(qkv, query_segment, key_segment):
    rows, width = qkv.shape
    width = width // 3
    blocks = width // LANES

    def kernel(q_ref, k_ref, v_ref, qs_ref, ks_ref, out_ref, lse_ref):
        allowed = ks_ref[...] == qs_ref[...]
        q = q_ref[...] * SCALE
        k = k_ref[...]
        v_t = v_ref[...].T
        lane = lax.broadcasted_iota(jnp.int32, (1, LANES), 1)
        outs = []
        for h in range(LANES // HEAD_DIM):
            k_h = jnp.where(lane // HEAD_DIM == h, k, jnp.zeros_like(k))
            scores = jnp.where(allowed, dot_nt(k_h, q), MASKED)
            top = jnp.max(scores, axis=0, keepdims=True)
            weight = jnp.exp(scores - top)
            total = jnp.sum(weight, axis=0, keepdims=True)
            probs = (weight * (1.0 / total)).astype(BF16)
            outs.append(dot_nn(v_t[h * HEAD_DIM : (h + 1) * HEAD_DIM], probs))
            lse_ref[0, h : h + 1, :] = top + jnp.log(total)
        out_ref[...] = jnp.concatenate(outs, axis=0).T.astype(BF16)

    return pl.pallas_call(
        kernel,
        out_shape=[
            jax.ShapeDtypeStruct((rows, width), BF16),
            jax.ShapeDtypeStruct((blocks, LANES // HEAD_DIM, rows), F32),
        ],
        grid=(blocks,),
        in_specs=[
            pl.BlockSpec((rows, LANES), lambda i: (0, i)),
            pl.BlockSpec((rows, LANES), lambda i: (0, blocks + i)),
            pl.BlockSpec((rows, LANES), lambda i: (0, 2 * blocks + i)),
            pl.BlockSpec((1, rows), lambda i: (0, 0)),
            pl.BlockSpec((rows, 1), lambda i: (0, 0)),
        ],
        out_specs=[
            pl.BlockSpec((rows, LANES), lambda i: (0, i)),
            pl.BlockSpec((1, LANES // HEAD_DIM, rows), lambda i: (i, 0, 0)),
        ],
        name="attend_forward",
    )(qkv, qkv, qkv, query_segment, key_segment)


def attend_backward(qkv, d_attn, lse, query_segment, key_segment):
    rows, width = d_attn.shape
    blocks = width // LANES

    def kernel(q_ref, k_ref, v_ref, d_ref, lse_ref, qs_ref, ks_ref, dq_ref, dk_ref, dv_ref):
        allowed = ks_ref[...] == qs_ref[...]
        q = q_ref[...] * SCALE
        k = k_ref[...]
        v = v_ref[...]
        d_out = d_ref[...]
        k_t = k.T
        lane = lax.broadcasted_iota(jnp.int32, (1, LANES), 1)
        d_q, d_k, d_v = [], 0.0, 0.0
        for h in range(LANES // HEAD_DIM):
            here = lane // HEAD_DIM == h
            zero = jnp.zeros_like(k)
            k_h = jnp.where(here, k, zero)
            scores = dot_nt(k_h, q)
            probs = jnp.where(allowed, jnp.exp(scores - lse_ref[0, h : h + 1, :]), 0.0)
            d_out_h = jnp.where(here, d_out, zero)
            d_v = d_v + dot_nn(probs.astype(BF16), d_out_h)
            d_probs = dot_nt(v, d_out_h)
            inner = jnp.sum(probs * d_probs, axis=0, keepdims=True)
            d_scores = (probs * (d_probs - inner)).astype(BF16)
            d_k = d_k + dot_nn(d_scores, jnp.where(here, q, zero))
            d_q.append(dot_nn(k_t[h * HEAD_DIM : (h + 1) * HEAD_DIM], d_scores))
        dq_ref[...] = (jnp.concatenate(d_q, axis=0).T * SCALE).astype(BF16)
        dk_ref[...] = d_k.astype(BF16)
        dv_ref[...] = d_v.astype(BF16)

    head = pl.BlockSpec((rows, LANES), lambda i: (0, i))
    return pl.pallas_call(
        kernel,
        out_shape=[jax.ShapeDtypeStruct((rows, width), BF16)] * 3,
        grid=(blocks,),
        in_specs=[
            head,
            pl.BlockSpec((rows, LANES), lambda i: (0, blocks + i)),
            pl.BlockSpec((rows, LANES), lambda i: (0, 2 * blocks + i)),
            head,
            pl.BlockSpec((1, LANES // HEAD_DIM, rows), lambda i: (i, 0, 0)),
            pl.BlockSpec((1, rows), lambda i: (0, 0)),
            pl.BlockSpec((rows, 1), lambda i: (0, 0)),
        ],
        out_specs=[head] * 3,
        name="attend_backward",
    )(qkv, qkv, qkv, d_attn, lse, query_segment, key_segment)


def normalize(stream):
    middle = jnp.mean(stream, axis=-1, keepdims=True)
    centered = stream - middle
    spread = jnp.mean(centered * centered, axis=-1, keepdims=True)
    rho = lax.rsqrt(spread + EPSILON)
    return centered * rho, rho


def normalize_back(grad, gain, hat, rho):
    scaled = grad * gain
    return rho * (
        scaled
        - jnp.mean(scaled, axis=-1, keepdims=True)
        - hat * jnp.mean(scaled * hat, axis=-1, keepdims=True)
    )


def gelu_tanh(values):
    return jax.nn.gelu(values, approximate=True)


def layout(lengths, row_count, tile_rows):
    tile_counts = (lengths + tile_rows - 1) // tile_rows
    seg_ends = jnp.cumsum(tile_counts) * tile_rows
    seg_starts = seg_ends - tile_counts * tile_rows
    position = jnp.arange(row_count, dtype=jnp.int32)[:, None]
    inside = (position >= seg_starts[None, :]) & (position < seg_ends[None, :])
    segment = jnp.sum((position >= seg_ends[None, :]).astype(jnp.int32), axis=1)
    offset = jnp.sum(jnp.where(inside, position - seg_starts[None, :], 0), axis=1)
    length_here = jnp.sum(jnp.where(inside, lengths[None, :], 0), axis=1)
    return (segment, offset < length_here)


def col_sums(values):
    return jnp.sum(values.astype(F32), axis=0)


def per_device(
    tokens,
    cotangent,
    tile_dest,
    seq_lengths,
    norm1_gain,
    norm1_bias,
    w_qkv,
    q_bias,
    v_bias,
    w_out,
    out_bias,
    norm2_gain,
    norm2_bias,
    w_up,
    up_bias,
    w_down,
    down_bias,
):
    dp_size = lax.axis_size("dp")
    peer_count = lax.axis_size("fsdp")
    cube = Cube(dp_size, peer_count)
    my_dp, my_fs = lax.axis_index("dp"), lax.axis_index("fsdp")
    me = jnp.stack([my_dp, my_fs]).astype(jnp.int32)
    tile_count = tile_dest.shape[0]
    row_count, width = tokens.shape
    tile_rows = row_count // tile_count
    shard = w_qkv.shape[0]
    hidden = w_up.shape[1]
    hidden_shard = w_down.shape[0]
    spread = hidden // width

    small = [norm1_gain, norm1_bias, q_bias, v_bias, out_bias, norm2_gain, norm2_bias, down_bias]
    dest_column = jnp.zeros((shard,), F32).at[:tile_count].set(tile_dest.astype(F32))
    columns = jnp.concatenate(
        [jnp.stack(small + [dest_column], axis=1), up_bias.reshape(shard, spread)], axis=1
    )
    columns = jnp.pad(columns, ((0, 0), (0, LANES - columns.shape[1])))
    chunk_a = jnp.concatenate([w_qkv, w_out, columns], axis=1).astype(BF16)
    width_a = chunk_a.shape[1]
    cut_a = (width_a // 2 + LANES - 1) // LANES * LANES

    target = tile_dest // tile_count
    peer_ids = jnp.arange(peer_count, dtype=jnp.int32)
    sending = target[None, :] == peer_ids[:, None]
    give_index = jnp.sum(
        jnp.where(sending, jnp.arange(tile_count, dtype=jnp.int32)[None, :], 0), axis=1
    )
    tiled = (tile_count, tile_rows, width)
    bucket_tokens, bucket_cot = pick_tiles(
        [tokens.reshape(tiled), cotangent.reshape(tiled)], give_index, peer_count
    )

    def exchange(buckets):
        return lax.all_to_all(buckets, "fsdp", split_axis=0, concat_axis=0, tiled=True)

    got_tokens = exchange(bucket_tokens)
    full_a = gather_parts(cube, chunk_a, (1, cut_a))
    got_cot = exchange(bucket_cot)
    full_b = gather_parts(cube, w_up.astype(BF16), (1, hidden // 2))
    full_c = gather_parts(cube, w_down.astype(BF16), (0, hidden_shard // 2))

    def column_plan(start, stop):
        pieces = []
        every = slice(None)
        if start < cut_a:
            end = min(stop, cut_a)
            pieces.append((0, (every, slice(start, end)), (every, slice(0, end - start))))
        if stop > cut_a:
            begin = max(start, cut_a)
            pieces.append(
                (
                    1,
                    (every, slice(begin - cut_a, stop - cut_a)),
                    (every, slice(begin - start, stop - start)),
                )
            )
        return pieces

    wide = 3 * width
    mat_qkv, mat_out, vectors = assemble(
        cube,
        full_a,
        me,
        [(shard, wide), (shard, width), (shard, LANES)],
        [column_plan(0, wide), column_plan(wide, wide + width), column_plan(wide + width, width_a)],
    )
    every = slice(None)
    half = hidden // 2
    (mat_up,) = assemble(
        cube,
        full_b,
        me,
        [(shard, hidden)],
        [
            [
                (0, (every, slice(0, half)), (every, slice(0, half))),
                (1, (every, slice(0, half)), (every, slice(half, hidden))),
            ]
        ],
    )
    half_rows = hidden_shard // 2
    (mat_down,) = assemble(
        cube,
        full_c,
        me,
        [(hidden_shard, width)],
        [
            [
                (0, (every, every), (slice(0, half_rows), every)),
                (1, (every, every), (slice(half_rows, hidden_shard), every)),
            ]
        ],
    )
    vectors = vectors.astype(F32)
    gain_one, shift_one, bias_q, bias_v, bias_out, gain_two, shift_two, bias_down, dest_all = (
        vectors[:, :9].T
    )
    bias_up = vectors[:, 9 : 9 + spread].reshape(hidden)

    dest_all = dest_all.reshape(dp_size, peer_count, shard)[:, :, :tile_count].astype(jnp.int32)
    dest_here = lax.dynamic_index_in_dim(dest_all, my_dp, 0, keepdims=False)
    to_me = dest_here // tile_count == my_fs
    got_slot = jnp.sum(jnp.where(to_me, dest_here % tile_count + 1, 0), axis=1) - 1
    slots = jnp.arange(tile_count, dtype=jnp.int32)
    take_index = jnp.sum(
        jnp.where(got_slot[None, :] == slots[:, None], peer_ids[None, :], 0), axis=1
    )
    back_index = jnp.maximum(got_slot, 0)

    (local_tokens,) = pick_tiles([got_tokens], take_index, tile_count)
    (local_cot,) = pick_tiles([got_cot], take_index, tile_count)
    local_tokens = local_tokens.reshape(row_count, width)
    local_cot = local_cot.reshape(row_count, width)

    segment, valid_rows = layout(seq_lengths[0], row_count, tile_rows)
    query_segment = segment[None, :]
    key_segment = jnp.where(valid_rows, segment, -1)[:, None]

    stream = local_tokens.astype(F32)
    hat_one, rho_one = normalize(stream)
    norm_one = (hat_one * gain_one + shift_one).astype(BF16)
    qkv_shift = jnp.concatenate([bias_q, jnp.zeros((width,), F32), bias_v])
    qkv_low = (dot_nn(norm_one, mat_qkv) + qkv_shift).astype(BF16)
    attn_out, lse = attend_forward(qkv_low, query_segment, key_segment)
    mid_stream = stream + dot_nn(attn_out, mat_out) + bias_out
    hat_two, rho_two = normalize(mid_stream)
    norm_two = (hat_two * gain_two + shift_two).astype(BF16)
    pre_act = dot_nn(norm_two, mat_up) + bias_up
    act_value, gelu_pull = jax.vjp(gelu_tanh, pre_act)
    act_low = act_value.astype(BF16)
    result = (mid_stream + dot_nn(act_low, mat_down) + bias_down).astype(BF16)

    def send_back(rows_low):
        (buckets,) = pick_tiles([rows_low.reshape(tiled)], back_index, peer_count)
        return exchange(buckets)

    def receive_back(got):
        (tiles,) = pick_tiles([got], target, tile_count)
        return tiles.reshape(row_count, width)

    mixed = receive_back(send_back(result))

    grad_out_rows = local_cot.astype(F32) * valid_rows.astype(F32)[:, None]
    grad_out_low = grad_out_rows.astype(BF16)
    d_down_bias = col_sums(grad_out_low)
    d_w_down = dot_tn(act_low, grad_out_low).astype(BF16)
    d_act = dot_nt(grad_out_low, mat_down)
    d_pre = gelu_pull(d_act)[0].astype(BF16)
    d_up_bias = col_sums(d_pre)
    d_w_up = dot_tn(norm_two, d_pre).astype(BF16)
    d_norm_two = dot_nt(d_pre, mat_up)
    d_gain_two = jnp.sum(d_norm_two * hat_two, axis=0)
    d_shift_two = jnp.sum(d_norm_two, axis=0)
    d_mid = grad_out_rows + normalize_back(d_norm_two, gain_two, hat_two, rho_two)
    d_proj_low = d_mid.astype(BF16)
    d_out_bias = col_sums(d_proj_low)
    d_w_out = dot_tn(attn_out, d_proj_low).astype(BF16)
    d_attn = dot_nt(d_proj_low, mat_out).astype(BF16)

    devices = dp_size * peer_count
    d_w_down = d_w_down.reshape(devices, 2, half_rows, width)
    s_down = scatter_sum(
        cube,
        [d_w_down[:, i].reshape(devices * half_rows, width) for i in range(2)],
        [half_rows, half_rows],
    )
    s_up = scatter_sum(cube, [d_w_up[:, :half], d_w_up[:, half:]], [shard, shard])

    d_q, d_k, d_v = attend_backward(qkv_low, d_attn, lse, query_segment, key_segment)
    d_qkv = jnp.concatenate([d_q, d_k, d_v], axis=1)
    d_q_bias = col_sums(d_q)
    d_v_bias = col_sums(d_v)
    d_w_qkv = dot_tn(norm_one, d_qkv).astype(BF16)
    d_norm_one = dot_nt(d_qkv, mat_qkv)
    d_gain_one = jnp.sum(d_norm_one * hat_one, axis=0)
    d_shift_one = jnp.sum(d_norm_one, axis=0)
    d_stream = d_mid + normalize_back(d_norm_one, gain_one, hat_one, rho_one)
    grad_tokens = receive_back(send_back(d_stream.astype(BF16)))

    d_small = [
        d_gain_one,
        d_shift_one,
        d_q_bias,
        d_v_bias,
        d_out_bias,
        d_gain_two,
        d_shift_two,
        d_down_bias,
    ]
    d_columns = jnp.concatenate(
        [jnp.stack(d_small, axis=1), d_up_bias.reshape(width, spread)], axis=1
    )
    d_columns = jnp.pad(d_columns, ((0, 0), (0, LANES - d_columns.shape[1]))).astype(BF16)
    d_chunk_a = jnp.concatenate([d_w_qkv, d_w_out, d_columns], axis=1)
    s_a = scatter_sum(cube, [d_chunk_a[:, :cut_a], d_chunk_a[:, cut_a:]], [shard, shard])
    s_a = jnp.concatenate(s_a, axis=1)
    s_columns = s_a[:, wide + width :]
    s_small = s_columns[:, :8].T
    return (
        mixed,
        grad_tokens,
        s_small[0],
        s_small[1],
        s_a[:, :wide],
        s_small[2],
        s_small[3],
        s_a[:, wide : wide + width],
        s_small[4],
        s_small[5],
        s_small[6],
        jnp.concatenate(s_up, axis=1),
        s_columns[:, 8 : 8 + spread].reshape(hidden_shard),
        jnp.concatenate(s_down, axis=0),
        s_small[7],
    )


def solution(mesh):
    rows, matrix = P(AXES), P(AXES, None)
    in_specs = (
        matrix,
        matrix,
        rows,
        matrix,
        rows,
        rows,
        matrix,
        rows,
        rows,
        matrix,
        rows,
        rows,
        rows,
        matrix,
        rows,
        matrix,
        rows,
    )
    out_specs = (
        matrix,
        matrix,
        rows,
        rows,
        matrix,
        rows,
        rows,
        matrix,
        rows,
        rows,
        rows,
        matrix,
        rows,
        matrix,
        rows,
    )
    return jax.shard_map(
        per_device, mesh=mesh, in_specs=in_specs, out_specs=out_specs, check_vma=False
    )
```

time: 876 us -> 463 us (0.53)
  waiting for transfers between devices: 377 us -> 165 us
  matrix products: 225 us -> 50.4 us
  blocking collectives: 121 us -> 0 us
  Pallas kernels: 0 us -> 92.3 us
  starting transfers between devices: 26.6 us -> 69.7 us
  local copies, waits for them, and re-layouts: 71.4 us -> 30.7 us
  other arithmetic: 27.3 us -> 45.4 us
  between operations: 15 us -> 2.14 us
    reduce_scatter x4 -> x0, waiting for transfers between devices: 240 us -> none  [the longest x1 142 us: per_device(): lax.psum_scatter(d_w_down, ('dp', 'fsdp'), scatter_dimension=0, tiled=True)]
    dot_general x104 -> x12, matrix products: 225 us -> 50.4 us  [the longest x4 17.7 us: dot_nn(): return jnp.dot(left, right, preferred_element_type=F32)]
    ppermute x0 -> x54, waiting for transfers between devices: none -> 151 us  [swap(): return lax.ppermute(value, axis, pairs)]
    unnamed x2 -> x0, blocking collectives: 121 us -> none
    pallas_call x0 -> x12, Pallas kernels: none -> 92.3 us  [the longest x3 34.3 us: assemble(): pl.pallas_call(kernel, out_shape=[jax.ShapeDtypeStruct((dp_high, 2, fs_si...]
    all_to_all x5 -> x4, waiting for transfers between devices: 80.3 us -> 14.1 us  [exchange(): lax.all_to_all(buckets, 'fsdp', split_axis=0, concat_axis=0, tiled=True)]
    all_gather x4 -> x0, waiting for transfers between devices: 56.8 us -> none  [the longest x1 56.7 us: per_device(): lax.all_gather(w_down.astype(jnp.bfloat16), ('dp', 'fsdp'), axis=0, tiled...]
    ppermute x0 -> x54, starting transfers between devices: none -> 49.4 us  [swap(): return lax.ppermute(value, axis, pairs)]
  transfers between devices with their start and end apart: 13 -> 58, of which waited for: 6 -> 24; matrix products, arithmetic and copies ran while one was open for 35% -> 16% of each run, Pallas kernels for 0% -> 17%
where the time goes in v1:
time: 463 us; the launch traced here: 455 us
  waiting for transfers between devices  165 us (36%)
  Pallas kernels  92.3 us (20%)
  starting transfers between devices  69.7 us (15%)
  matrix products  50.4 us (11%)
  other arithmetic  45.4 us (10%)
  local copies, waits for them, and re-layouts  30.7 us (7%)
    ppermute x54, waiting for transfers between devices, swap(): return lax.ppermute(value, axis, pairs)  151 us
    ppermute x54, starting transfers between devices, swap(): return lax.ppermute(value, axis, pairs)  49.4 us
    pallas_call x3, Pallas kernels, assemble(): pl.pallas_call(kernel, out_shape=[jax.ShapeDtypeStruct((dp_high, 2, fs_si...  34.3 us
    pallas_call x7, Pallas kernels, pick_tiles(): pl.pallas_call(kernel, out_shape=[jax.ShapeDtypeStruct((count,) + shape,...  33.7 us
    all_to_all x4, starting transfers between devices, exchange(): lax.all_to_all(buckets, 'fsdp', split_axis=0, concat_axis=0, tiled=True)  20.3 us
    dot_general x4, matrix products, dot_nn(): return jnp.dot(left, right, preferred_element_type=F32)  17.7 us
    dot_general x4, matrix products, dot_nt(): lax.dot_general(left, right, (((1,), (1,)), ((), ())), preferred_element_...  17.6 us
    dot_general x4, matrix products, dot_tn(): lax.dot_general(left, right, (((0,), (0,)), ((), ())), preferred_element_...  15.1 us
  transfers between devices with their start and end apart: 58, of which 24 were waited for; matrix products, arithmetic and copies ran while one was open for 16% of the time, Pallas kernels for 17%

profile of v1, /device:TPU:0, one launch (start us, length us, event | category | flops | bytes accessed | tf_op | source)
XLA Modules:
  0.0 455.3 jit_solution(2747884019641609941)
XLA Ops:
  10.3 3.1 collective-permute-start
  14.5 3.7 collective-permute-done
  18.3 3.0 collective-permute-start.1
  23.7 9.8 %collective-permute-done.1 = bf16[2,24,3200]{2,1,0:T(8,128)(2,1)S(1)} collective-permute-done((bf16[2,24,3200]{2,1,0:T(8,128)(2,1)S(1)}, bf16[2,24,3200]{2,1,0:T(8,128)(2,1)S(1)}, u32[]{:S(2)}, u32[]{:S(2)}) %collective-permute-start.1) | collective-permute-done | bytes 307232 | tf_op jit(solution)/shard_map/ppermute | solution.py:40
  36.8 3.9 collective-permute-done.5
  41.9 1.8 collective-permute-done.2
  44.9 14.3 %collective-permute-done.17 = bf16[2,96,768]{2,1,0:T(8,128)(2,1)S(1)} collective-permute-done((bf16[2,96,768]{2,1,0:T(8,128)(2,1)S(1)}, bf16[2,96,768]{2,1,0:T(8,128)(2,1)S(1)}, u32[]{:S(2)}, u32[]{:S(2)}) %collective-permute-start.17) | collective-permute-done | bytes 294944 | tf_op jit(solution)/shard_map/ppermute | solution.py:40
  64.2 6.1 %collective-permute-done.18 = bf16[4,48,768]{2,1,0:T(8,128)(2,1)S(1)} collective-permute-done((bf16[4,48,768]{2,1,0:T(8,128)(2,1)S(1)}, bf16[4,48,768]{2,1,0:T(8,128)(2,1)S(1)}, u32[]{:S(2)}, u32[]{:S(2)}) %collective-permute-start.18) | collective-permute-done | bytes 294944 | tf_op jit(solution)/shard_map/ppermute | solution.py:40
  75.7 11.5 %assemble.3 = (bf16[2,2,8,24,2304]{4,3,2,1,0:T(8,128)(2,1)}, bf16[2,2,8,24,768]{4,3,2,1,0:T(8,128)(2,1)}, bf16[2,2,8,24,128]{4,3,2,1,0:T(8,128)(2,1)}) custom-call(s32[2]{0:T(128)} %pad_add_fusion.me_ref, bf16[16,24,1664]{2,1,0:T(8,128)(2,1)} %copy-done.8, bf16[16,24,1664]{2,1,0:T(8,128)(2,1)} %collective-permute-done.4.other_p, ...), custom_call_target="tpu_custom_call" | custom-call | tf_op jit(solution)/shard_map/assemble/pallas_call | solution.py:90
  89.2 6.5 %pick_tiles.7 = (bf16[8,128,768]{2,1,0:T(8,128)(2,1)}, bf16[8,128,768]{2,1,0:T(8,128)(2,1)}) custom-call(s32[8]{0:T(128)} %get-tuple-element.119.index_ref, bf16[4,128,768]{2,1,0:T(8,128)(2,1)} %bitcast.353, bf16[4,128,768]{2,1,0:T(8,128)(2,1)} %bitcast.354), custom_call_target="tpu_custom_call" | custom-call | tf_op jit(solution)/shard_map/pick_tiles/pallas_call | solution.py:142
  95.6 5.1 %all-to-all-start = ((bf16[8,128,768]{2,1,0:T(8,128)(2,1)}), bf16[8,128,768]{2,1,0:T(8,128)(2,1)S(1)}, u32[]{:S(2)}, u32[]{:S(2)}) async-start(bf16[8,128,768]{2,1,0:T(8,128)(2,1)} %get-tuple-element.38), calls=%async_computation | async-start | bytes 3145728 | tf_op jit(solution)/shard_map/all_to_all | solution.py:357
  100.7 1.9 pad_maximum_fusion.11
  102.7 2.0 collective-permute-start.11
  104.7 1.9 pad_maximum_fusion.12
  108.7 2.7 pad_maximum_fusion.6.own_q
  111.5 19.7 %collective-permute-done.11 = bf16[8,24,1536]{2,1,0:T(8,128)(2,1)} collective-permute-done((bf16[8,24,1536]{2,1,0:T(8,128)(2,1)}, bf16[8,24,1536]{2,1,0:T(8,128)(2,1)}, u32[]{:S(2)}, u32[]{:S(2)}) %collective-permute-start.11) | collective-permute-done | bytes 589856 | tf_op jit(solution)/shard_map/ppermute | solution.py:40
  131.2 2.4 pad_maximum_fusion.3.own_p
  133.6 2.4 pad_maximum_fusion.4.own_q
  137.5 11.4 %assemble.5 = bf16[2,2,8,96,768]{4,3,2,1,0:T(8,128)(2,1)} custom-call(s32[2]{0:T(128)} %pad_add_fusion.me_ref, bf16[16,48,768]{2,1,0:T(8,128)(2,1)} %copy-done.9, bf16[16,48,768]{2,1,0:T(8,128)(2,1)} %collective-permute-done.20.other_p, bf16[16,48,768]{2,1,0:T(8,128)(2,1)} %pad_maximum_fusion.6.own_q, bf16[16,48,768]{2,1,0:T(8,128)(2,1)} %collective-permute-done.23.other_q), custom_call_target="tpu_custom_call" | custom-call | tf_op jit(solution)/shard_map/assemble/pallas_call | solution.py:90
  148.9 11.4 %assemble.4 = bf16[2,2,8,24,3072]{4,3,2,1,0:T(8,128)(2,1)} custom-call(s32[2]{0:T(128)} %pad_add_fusion.me_ref, bf16[16,24,1536]{2,1,0:T(8,128)(2,1)} %pad_maximum_fusion.3.own_p, bf16[16,24,1536]{2,1,0:T(8,128)(2,1)} %collective-permute-done.12.other_p, bf16[16,24,1536]{2,1,0:T(8,128)(2,1)} %pad_maximum_fusion.4.own_q, ...), custom_call_target="tpu_custom_call" | custom-call | tf_op jit(solution)/shard_map/assemble/pallas_call | solution.py:90
  162.4 5.1 %all-to-all-start.2 = ((bf16[8,128,768]{2,1,0:T(8,128)(2,1)}), bf16[8,128,768]{2,1,0:T(8,128)(2,1)S(1)}, u32[]{:S(2)}, u32[]{:S(2)}) async-start(bf16[8,128,768]{2,1,0:T(8,128)(2,1)} %get-tuple-element.42), calls=%async_computation.2 | async-start | bytes 3145728 | tf_op jit(solution)/shard_map/all_to_all | solution.py:357
  168.1 3.9 pick_tiles.8
  175.3 5.4 %fusion.8.q_ref.k_ref.v_ref = bf16[512,2304]{1,0:T(8,128)(2,1)} fusion(bf16[512,768]{1,0:T(8,128)(2,1)S(1)} %bitcast.356, bf16[768,2304]{1,0:T(8,128)(2,1)} %bitcast.363, f32[2304]{0:T(1024)S(1)} %pad_maximum_fusion.24), kind=kOutput, calls=%fused_computation.16 | convolution fusion | flops 1814298624 | bytes 6693888 | tf_op jit(solution)/shard_map/dot_general | solution.py:161
  180.8 10.4 %attend_forward.1 = (bf16[512,768]{1,0:T(8,128)(2,1)}, f32[6,2,512]{2,1,0:T(2,128)}) custom-call(bf16[512,2304]{1,0:T(8,128)(2,1)} %fusion.8.q_ref.k_ref.v_ref, bf16[512,2304]{1,0:T(8,128)(2,1)} %fusion.8.q_ref.k_ref.v_ref, bf16[512,2304]{1,0:T(8,128)(2,1)} %fusion.8.q_ref.k_ref.v_ref, s32[1,512]{1,0:T(1,128)} %bitcast.358, s32[512,1]{1,0:T(8,128)} %copy.123.ks_ref), custom_call_target="tpu_custom_call" | custom-call | tf_op jit(solution)/shard_map/attend_forward/pallas_call | solution.py:195
  191.2 2.4 fusion.79
  194.7 9.9 %all-to-all-done.2.refs_0_ = bf16[8,128,768]{2,1,0:T(8,128)(2,1)S(1)} async-done(((bf16[8,128,768]{2,1,0:T(8,128)(2,1)}), bf16[8,128,768]{2,1,0:T(8,128)(2,1)S(1)}, u32[]{:S(2)}, u32[]{:S(2)}) %all-to-all-start.2) | async-done | bytes 1572896 | tf_op jit(solution)/shard_map/all_to_all | solution.py:357
  205.8 3.9 pick_tiles.11
  211.4 5.0 %fusion.68 = f32[512,3072]{1,0:T(8,128)S(1)} fusion(bf16[768,3072]{1,0:T(8,128)(2,1)} %bitcast.338, f32[512,768]{1,0:T(8,128)S(1)} %copy-done.7, f32[768]{0:T(1024)S(1)} %get-tuple-element.57, f32[768]{0:T(1024)S(1)} %get-tuple-element.55, f32[512]{0:T(512)S(1)} %add_rsqrt_fusion, f32[512]{0:T(512)S(1)} %broadcast_multiply_fusion.4), kind=kOutput, calls=%fused_computation.276 | convolution fusion | flops 2417885184 | bytes 12593152 | tf_op jit(solution)/shard_map/dot_general | solution.py:161
  216.4 6.8 %fusion.69 = (bf16[3072]{0:T(1024)(128)(2,1)S(1)}, bf16[512,3072]{1,0:T(8,128)(2,1)S(1)}) fusion(f32[512,3072]{1,0:T(8,128)S(1)} %fusion.68, f32[3072]{0:T(1024)S(1)} %add.366, bf16[512,768]{1,0:T(8,128)(2,1)S(1)} %bitcast.355, bf16[3072,768]{1,0:T(8,128)(2,1)S(1)} %bitcast.336), kind=kOutput, calls=%fused_computation.277 | convolution fusion | flops 2450519040 | bytes 14960640 | tf_op jit(solution)/shard_map/dot_general | solution.py:169
  223.3 3.1 multiply_reduce_fusion
  229.3 1.9 convolution_convert_fusion.3
  231.3 4.9 %convolution_convert_fusion.1 = bf16[768,3072]{1,0:T(8,128)(2,1)} fusion(bf16[512,3072]{1,0:T(8,128)(2,1)S(1)} %get-tuple-element.76, f32[512,768]{1,0:T(8,128)S(1)} %copy-done.7, f32[768]{0:T(1024)S(1)} %get-tuple-element.57, f32[768]{0:T(1024)S(1)} %get-tuple-element.55, f32[512]{0:T(512)S(1)} %add_rsqrt_fusion, f32[512]{0:T(512)S(1)} %broadcast_multiply_fusion.4), kind=kOutput, calls=%fused_computation.11 | convolution fusion | flops 2420244480 | bytes 9447424 | tf_op jit(solution)/shard_map/dot_general | solution.py:165
  237.2 4.9 %add_convert_fusion = bf16[512,768]{1,0:T(8,128)(2,1)} fusion(f32[512,768]{1,0:T(8,128)S(1)} %copy-done.7, bf16[3072,768]{1,0:T(8,128)(2,1)S(1)} %bitcast.337, f32[768]{0:T(1024)S(1)} %get-tuple-element.56, f32[512,3072]{1,0:T(8,128)S(1)} %fusion.68, f32[3072]{0:T(1024)S(1)} %add.366), kind=kOutput, calls=%fused_computation.60 | convolution fusion | flops 2432827392 | bytes 13384704 | tf_op jit(solution)/shard_map/dot_general | solution.py:161
  242.1 5.8 %pick_tiles.9 = bf16[8,128,768]{2,1,0:T(8,128)(2,1)} custom-call(s32[8]{0:T(128)} %get-tuple-element.111.index_ref, bf16[4,128,768]{2,1,0:T(8,128)(2,1)} %bitcast.352), custom_call_target="tpu_custom_call" | custom-call | tf_op jit(solution)/shard_map/pick_tiles/pallas_call | solution.py:142
  247.9 4.5 all-to-all-start.1
  252.4 13.8 %attend_backward.1 = (bf16[512,768]{1,0:T(8,128)(2,1)}, bf16[512,768]{1,0:T(8,128)(2,1)}, bf16[512,768]{1,0:T(8,128)(2,1)}) custom-call(bf16[512,2304]{1,0:T(8,128)(2,1)} %fusion.8.q_ref.k_ref.v_ref, bf16[512,2304]{1,0:T(8,128)(2,1)} %fusion.8.q_ref.k_ref.v_ref, bf16[512,2304]{1,0:T(8,128)(2,1)} %fusion.8.q_ref.k_ref.v_ref, ...), custom_call_target="tpu_custom_call" | custom-call | tf_op jit(solution)/shard_map/attend_backward/pallas_call | solution.py:248
  268.0 6.0 %fusion.35 = (bf16[768]{0:T(1024)(128)(2,1)S(1)}, f32[512]{0:T(512)S(1)}, f32[512]{0:T(512)S(1)}, bf16[768]{0:T(1024)(128)(2,1)S(1)}, bf16[512,768]{1,0:T(8,128)(2,1)}, /*index=5*/f32[512,768]{1,0:T(8,128)S(1)}) fusion(bf16[4,128,768]{2,1,0:T(8,128)(2,1)S(1)} %copy-done, f32[512]{0:T(512)S(1)} %get-tuple-element.108, f32[512]{0:T(512)S(1)} %get-tuple-element.106, ...), kind=kOutput, calls=%fused_computation.55 | convolution fusion | flops 1817048576 | bytes 9061376 | tf_op jit(solution)/shard_map/dot_general | solution.py:169
  275.5 5.8 %pick_tiles.12 = bf16[8,128,768]{2,1,0:T(8,128)(2,1)} custom-call(s32[8]{0:T(128)} %get-tuple-element.111.index_ref, bf16[4,128,768]{2,1,0:T(8,128)(2,1)} %bitcast.344), custom_call_target="tpu_custom_call" | custom-call | tf_op jit(solution)/shard_map/pick_tiles/pallas_call | solution.py:142
  289.1 3.9 convolution_convert_fusion.2
  293.1 3.7 concatenate.133
  304.9 4.4 convolution_convert_fusion
  313.9 2.0 collective-permute-start.35
  317.8 9.5 %collective-permute-done.25 = bf16[2,2,2,24,1536]{4,3,1,0,2:T(8,128)(2,1)S(1)} collective-permute-done((bf16[2,2,2,24,1536]{4,3,1,0,2:T(8,128)(2,1)S(1)}, bf16[2,2,2,24,1536]{4,3,1,0,2:T(8,128)(2,1)S(1)}, u32[]{:S(2)}, u32[]{:S(2)}) %collective-permute-start.25) | collective-permute-done | bytes 589856 | tf_op jit(solution)/shard_map/ppermute | solution.py:40
  327.3 1.9 collective-permute-start.30
  329.3 10.5 %collective-permute-done.40 = bf16[2,2,2,24,1536]{4,3,1,0,2:T(8,128)(2,1)S(1)} collective-permute-done((bf16[2,2,2,24,1536]{4,3,1,0,2:T(8,128)(2,1)S(1)}, bf16[2,2,2,24,1536]{4,3,1,0,2:T(8,128)(2,1)S(1)}, u32[]{:S(2)}, u32[]{:S(2)}) %collective-permute-start.40) | collective-permute-done | bytes 589856 | tf_op jit(solution)/shard_map/ppermute | solution.py:40
  339.9 1.9 collective-permute-start.26
  342.4 9.2 %collective-permute-done.50 = bf16[2,2,2,48,768]{4,3,1,0,2:T(8,128)(2,1)S(1)} collective-permute-done((bf16[2,2,2,48,768]{4,3,1,0,2:T(8,128)(2,1)S(1)}, bf16[2,2,2,48,768]{4,3,1,0,2:T(8,128)(2,1)S(1)}, u32[]{:S(2)}, u32[]{:S(2)}) %collective-permute-start.50) | collective-permute-done | bytes 589856 | tf_op jit(solution)/shard_map/ppermute | solution.py:40
  352.3 2.0 collective-permute-start.51
  354.5 2.0 collective-permute-done.30
  357.2 5.6 %collective-permute-done.26 = bf16[2,2,24,1536]{3,2,1,0:T(8,128)(2,1)S(1)} collective-permute-done((bf16[2,2,24,1536]{3,2,1,0:T(8,128)(2,1)S(1)}, bf16[2,2,24,1536]{3,2,1,0:T(8,128)(2,1)S(1)}, u32[]{:S(2)}, u32[]{:S(2)}) %collective-permute-start.26) | collective-permute-done | bytes 294944 | tf_op jit(solution)/shard_map/ppermute | solution.py:40
  363.4 5.7 %collective-permute-done.41 = bf16[2,2,24,1536]{3,2,1,0:T(8,128)(2,1)S(1)} collective-permute-done((bf16[2,2,24,1536]{3,2,1,0:T(8,128)(2,1)S(1)}, bf16[2,2,24,1536]{3,2,1,0:T(8,128)(2,1)S(1)}, u32[]{:S(2)}, u32[]{:S(2)}) %collective-permute-start.41) | collective-permute-done | bytes 294944 | tf_op jit(solution)/shard_map/ppermute | solution.py:40
  369.1 2.9 collective-permute-start.27
  374.1 2.9 collective-permute-start.37
  377.4 10.3 %collective-permute-done.27 = bf16[2,24,1536]{2,1,0:T(8,128)(2,1)S(1)} collective-permute-done((bf16[2,24,1536]{2,1,0:T(8,128)(2,1)S(1)}, bf16[2,24,1536]{2,1,0:T(8,128)(2,1)S(1)}, u32[]{:S(2)}, u32[]{:S(2)}) %collective-permute-start.27) | collective-permute-done | bytes 147488 | tf_op jit(solution)/shard_map/ppermute | solution.py:40
  387.8 3.1 collective-permute-done.42
  390.9 2.6 collective-permute-start.28
  393.6 3.7 collective-permute-done.37
  397.3 3.0 collective-permute-done.52
  407.2 5.6 %all-to-all-start.3 = ((bf16[8,128,768]{2,1,0:T(8,128)(2,1)}), bf16[8,128,768]{2,1,0:T(8,128)(2,1)S(1)}, u32[]{:S(2)}, u32[]{:S(2)}) async-start(bf16[8,128,768]{2,1,0:T(8,128)(2,1)} %pick_tiles.12), calls=%async_computation.3 | async-start | bytes 3145728 | tf_op jit(solution)/shard_map/all_to_all | solution.py:357
  415.1 2.1 collective-permute-start.33
  418.0 23.1 %collective-permute-done.33 = bf16[24,1664]{1,0:T(8,128)(2,1)S(1)} collective-permute-done((bf16[24,1664]{1,0:T(8,128)(2,1)S(1)}, bf16[24,1664]{1,0:T(8,128)(2,1)S(1)}, u32[]{:S(2)}, u32[]{:S(2)}) %collective-permute-start.33) | collective-permute-done | bytes 79904 | tf_op jit(solution)/shard_map/ppermute | solution.py:40
  441.8 3.9 pick_tiles.10
  445.7 4.2 all-to-all-done.3.refs_0_
  451.1 3.9 pick_tiles.13
  (330 shorter events, 91.4 us)
Async XLA Ops:
  0.6 20.6 %copy-start.20 = (f32[24,3072]{1,0:T(8,128)S(1)}, f32[24,3072]{1,0:T(8,128)}, u32[]{:S(2)}) copy-start(f32[24,3072]{1,0:T(8,128)} %param.32) | copy-start | bytes 884740
  1.4 87.2 %copy-start.23 = (s32[4]{0:T(128)}, s32[4]{0:T(128)S(1)}, u32[]{:S(2)}) copy-start(s32[4]{0:T(128)S(1)} %get-tuple-element.113.index_ref) | copy-start | bytes 52
  10.3 7.9 %collective-permute-start = (bf16[1,24,3200]{2,1,0:T(8,128)(2,1)S(1)}, bf16[1,24,3200]{2,1,0:T(8,128)(2,1)S(1)}, u32[]{:S(2)}, u32[]{:S(2)}) collective-permute-start(bf16[1,24,3200]{2,1,0:T(8,128)(2,1)S(1)} %pad_maximum_fusion.23), channel_id=1, source_target_pairs={{0,2},{1,3},{2,0},{3,1},{4,6},{5,7},{6,4},{7,5},{8,10},{9,11},{10,... | collective-permute-start | bytes 460808 | tf_op jit(solution)/shard_map/ppermute | solution.py:40
  14.4 22.2 %collective-permute-start.16 = (bf16[1,96,768]{2,1,0:T(8,128)(2,1)S(1)}, bf16[1,96,768]{2,1,0:T(8,128)(2,1)S(1)}, u32[]{:S(2)}, u32[]{:S(2)}) collective-permute-start(bf16[1,96,768]{2,1,0:T(8,128)(2,1)S(1)} %convert_bitcast_fusion), channel_id=1, source_target_pairs={{0,2},{1,3},{2,0},{3,1},{4,6},{5,7},{6,4},{7,5},{8,10},{9,11},{10,... | collective-permute-start | bytes 442376 | tf_op jit(solution)/shard_map/ppermute | solution.py:40
  18.3 15.2 %collective-permute-start.1 = (bf16[2,24,3200]{2,1,0:T(8,128)(2,1)S(1)}, bf16[2,24,3200]{2,1,0:T(8,128)(2,1)S(1)}, u32[]{:S(2)}, u32[]{:S(2)}) collective-permute-start(bf16[2,24,3200]{2,1,0:T(8,128)(2,1)S(1)} %pad_maximum_fusion.16), channel_id=1, source_target_pairs={{0,4},{1,5},{2,6},{3,7},{4,0},{5,1},{6,2},{7,3},{8,12},{9,13},{10,... | collective-permute-start | bytes 921608 | tf_op jit(solution)/shard_map/ppermute | solution.py:40
  21.3 23.5 %collective-permute-start.8 = (bf16[1,24,3072]{2,1,0:T(8,128)(2,1)S(1)}, bf16[1,24,3072]{2,1,0:T(8,128)(2,1)S(1)}, u32[]{:S(2)}, u32[]{:S(2)}) collective-permute-start(bf16[1,24,3072]{2,1,0:T(8,128)(2,1)S(1)} %convert_bitcast_fusion.1), channel_id=1, source_target_pairs={{0,2},{1,3},{2,0},{3,1},{4,6},{5,7},{6,4},{7,5},{8,10},{9,11},{10,... | collective-permute-start | bytes 442376 | tf_op jit(solution)/shard_map/ppermute | solution.py:40
  33.5 7.1 %collective-permute-start.5 = (bf16[4,24,1536]{2,1,0:T(8,128)(2,1)S(1)}, bf16[4,24,1536]{2,1,0:T(8,128)(2,1)S(1)}, u32[]{:S(2)}, u32[]{:S(2)}) collective-permute-start(bf16[4,24,1536]{2,1,0:T(8,128)(2,1)S(1)} %pad_maximum_fusion.17), channel_id=1, source_target_pairs={{0,1},{1,0},{2,3},{3,2},{4,5},{5,4},{6,7},{7,6},{8,9},{9,8},{10,11... | collective-permute-start | bytes 884744 | tf_op jit(solution)/shard_map/ppermute | solution.py:40
  35.1 8.6 %collective-permute-start.2 = (bf16[4,24,1664]{2,1,0:T(8,128)(2,1)S(1)}, bf16[4,24,1664]{2,1,0:T(8,128)(2,1)S(1)}, u32[]{:S(2)}, u32[]{:S(2)}) collective-permute-start(bf16[4,24,1664]{2,1,0:T(8,128)(2,1)S(1)} %slice.122), channel_id=1, source_target_pairs={{0,16},{8,24},{16,0},{24,8},{1,17},{9,25},{17,1},{25,9},{2,18},{10... | collective-permute-start | bytes 958472 | tf_op jit(solution)/shard_map/ppermute | solution.py:40
  36.7 22.5 %collective-permute-start.17 = (bf16[2,96,768]{2,1,0:T(8,128)(2,1)S(1)}, bf16[2,96,768]{2,1,0:T(8,128)(2,1)S(1)}, u32[]{:S(2)}, u32[]{:S(2)}) collective-permute-start(bf16[2,96,768]{2,1,0:T(8,128)(2,1)S(1)} %pad_maximum_fusion.19), channel_id=1, source_target_pairs={{0,4},{1,5},{2,6},{3,7},{4,0},{5,1},{6,2},{7,3},{8,12},{9,13},{10,... | collective-permute-start | bytes 884744 | tf_op jit(solution)/shard_map/ppermute | solution.py:40
  40.7 18.6 %collective-permute-start.6 = (bf16[8,24,1536]{2,1,0:T(8,128)(2,1)S(1)}, bf16[8,24,1536]{2,1,0:T(8,128)(2,1)S(1)}, u32[]{:S(2)}, u32[]{:S(2)}) collective-permute-start(bf16[8,24,1536]{2,1,0:T(8,128)(2,1)S(1)} %pad_maximum_fusion.9), channel_id=1, source_target_pairs={{0,16},{8,24},{16,0},{24,8},{1,17},{9,25},{17,1},{25,9},{2,18},{10... | collective-permute-start | bytes 1769480 | tf_op jit(solution)/shard_map/ppermute | solution.py:40
  43.8 15.7 %collective-permute-start.3 = (bf16[8,24,1664]{2,1,0:T(8,128)(2,1)S(1)}, bf16[8,24,1664]{2,1,0:T(8,128)(2,1)S(1)}, u32[]{:S(2)}, u32[]{:S(2)}) collective-permute-start(bf16[8,24,1664]{2,1,0:T(8,128)(2,1)S(1)} %pad_maximum_fusion.7), channel_id=1, source_target_pairs={{0,1},{1,0},{2,3},{3,2},{4,5},{5,4},{6,7},{7,6},{8,9},{9,8},{10,11... | collective-permute-start | bytes 1916936 | tf_op jit(solution)/shard_map/ppermute | solution.py:40
  44.8 18.0 %collective-permute-start.9 = (bf16[2,24,3072]{2,1,0:T(8,128)(2,1)S(1)}, bf16[2,24,3072]{2,1,0:T(8,128)(2,1)S(1)}, u32[]{:S(2)}, u32[]{:S(2)}) collective-permute-start(bf16[2,24,3072]{2,1,0:T(8,128)(2,1)S(1)} %pad_maximum_fusion.18), channel_id=1, source_target_pairs={{0,4},{1,5},{2,6},{3,7},{4,0},{5,1},{6,2},{7,3},{8,12},{9,13},{10,... | collective-permute-start | bytes 884744 | tf_op jit(solution)/shard_map/ppermute | solution.py:40
  59.4 14.8 %collective-permute-start.7 = (bf16[16,24,1536]{2,1,0:T(8,128)(2,1)S(1)}, bf16[16,24,1536]{2,1,0:T(8,128)(2,1)S(1)}, u32[]{:S(2)}, u32[]{:S(2)}) collective-permute-start(bf16[16,24,1536]{2,1,0:T(8,128)(2,1)S(1)} %pad_maximum_fusion.2.own_q), channel_id=1, source_target_pairs={{0,8},{8,0},{16,24},{24,16},{1,9},{9,1},{17,25},{25,17},{2,10},{10... | collective-permute-start | bytes 3538952 | tf_op jit(solution)/shard_map/ppermute | solution.py:40
  59.7 16.1 %collective-permute-start.4 = (bf16[16,24,1664]{2,1,0:T(8,128)(2,1)S(1)}, bf16[16,24,1664]{2,1,0:T(8,128)(2,1)}, u32[]{:S(2)}, u32[]{:S(2)}) collective-permute-start(bf16[16,24,1664]{2,1,0:T(8,128)(2,1)S(1)} %pad_maximum_fusion.1.own_p), channel_id=1, source_target_pairs={{0,8},{8,0},{16,24},{24,16},{1,9},{9,1},{17,25},{25,17},{2,10},{10... | collective-permute-start | bytes 3833864 | tf_op jit(solution)/shard_map/ppermute | solution.py:40
  60.4 12.8 %copy-start.11 = (bf16[4,48,768]{2,1,0:T(8,128)(2,1)}, bf16[4,48,768]{2,1,0:T(8,128)(2,1)S(1)}, u32[]{:S(2)}) copy-start(bf16[4,48,768]{2,1,0:T(8,128)(2,1)S(1)} %get-tuple-element.104) | copy-start | bytes 884740
  60.4 9.9 %collective-permute-start.18 = (bf16[4,48,768]{2,1,0:T(8,128)(2,1)S(1)}, bf16[4,48,768]{2,1,0:T(8,128)(2,1)S(1)}, u32[]{:S(2)}, u32[]{:S(2)}) collective-permute-start(bf16[4,48,768]{2,1,0:T(8,128)(2,1)S(1)} %get-tuple-element.105), channel_id=1, source_target_pairs={{0,16},{8,24},{16,0},{24,8},{1,17},{9,25},{17,1},{25,9},{2,18},{10... | collective-permute-start | bytes 884744 | tf_op jit(solution)/shard_map/ppermute | solution.py:40
  61.0 10.7 %collective-permute-start.21 = (bf16[4,48,768]{2,1,0:T(8,128)(2,1)S(1)}, bf16[4,48,768]{2,1,0:T(8,128)(2,1)S(1)}, u32[]{:S(2)}, u32[]{:S(2)}) collective-permute-start(bf16[4,48,768]{2,1,0:T(8,128)(2,1)S(1)} %get-tuple-element.104), channel_id=1, source_target_pairs={{0,1},{1,0},{2,3},{3,2},{4,5},{5,4},{6,7},{7,6},{8,9},{9,8},{10,11... | collective-permute-start | bytes 884744 | tf_op jit(solution)/shard_map/ppermute | solution.py:40
  63.7 37.1 %collective-permute-start.10 = (bf16[4,24,1536]{2,1,0:T(8,128)(2,1)}, bf16[4,24,1536]{2,1,0:T(8,128)(2,1)}, u32[]{:S(2)}, u32[]{:S(2)}) collective-permute-start(bf16[4,24,1536]{2,1,0:T(8,128)(2,1)} %get-tuple-element.103), channel_id=1, source_target_pairs={{0,16},{8,24},{16,0},{24,8},{1,17},{9,25},{17,1},{25,9},{2,18},{10... | collective-permute-start | bytes 884744 | tf_op jit(solution)/shard_map/ppermute | solution.py:40
  70.3 34.4 %collective-permute-start.13 = (bf16[4,24,1536]{2,1,0:T(8,128)(2,1)S(1)}, bf16[4,24,1536]{2,1,0:T(8,128)(2,1)}, u32[]{:S(2)}, u32[]{:S(2)}) collective-permute-start(bf16[4,24,1536]{2,1,0:T(8,128)(2,1)S(1)} %get-tuple-element.102), channel_id=1, source_target_pairs={{0,1},{1,0},{2,3},{3,2},{4,5},{5,4},{6,7},{7,6},{8,9},{9,8},{10,11... | collective-permute-start | bytes 884744 | tf_op jit(solution)/shard_map/ppermute | solution.py:40
  71.7 35.5 %collective-permute-start.19 = (bf16[8,48,768]{2,1,0:T(8,128)(2,1)}, bf16[8,48,768]{2,1,0:T(8,128)(2,1)}, u32[]{:S(2)}, u32[]{:S(2)}) collective-permute-start(bf16[8,48,768]{2,1,0:T(8,128)(2,1)} %pad_maximum_fusion.14), channel_id=1, source_target_pairs={{0,1},{1,0},{2,3},{3,2},{4,5},{5,4},{6,7},{7,6},{8,9},{9,8},{10,11... | collective-permute-start | bytes 1769480 | tf_op jit(solution)/shard_map/ppermute | solution.py:40
  75.2 33.5 %collective-permute-start.22 = (bf16[8,48,768]{2,1,0:T(8,128)(2,1)}, bf16[8,48,768]{2,1,0:T(8,128)(2,1)}, u32[]{:S(2)}, u32[]{:S(2)}) collective-permute-start(bf16[8,48,768]{2,1,0:T(8,128)(2,1)} %pad_maximum_fusion.15), channel_id=1, source_target_pairs={{0,16},{8,24},{16,0},{24,8},{1,17},{9,25},{17,1},{25,9},{2,18},{10... | collective-permute-start | bytes 1769480 | tf_op jit(solution)/shard_map/ppermute | solution.py:40
  95.6 65.6 %all-to-all-start = ((bf16[8,128,768]{2,1,0:T(8,128)(2,1)}), bf16[8,128,768]{2,1,0:T(8,128)(2,1)S(1)}, u32[]{:S(2)}, u32[]{:S(2)}) async-start(bf16[8,128,768]{2,1,0:T(8,128)(2,1)} %get-tuple-element.38), calls=%async_computation | async-start | bytes 3145728 | tf_op jit(solution)/shard_map/all_to_all | solution.py:357
  102.7 28.5 %collective-permute-start.11 = (bf16[8,24,1536]{2,1,0:T(8,128)(2,1)}, bf16[8,24,1536]{2,1,0:T(8,128)(2,1)}, u32[]{:S(2)}, u32[]{:S(2)}) collective-permute-start(bf16[8,24,1536]{2,1,0:T(8,128)(2,1)} %pad_maximum_fusion.11), channel_id=1, source_target_pairs={{0,1},{1,0},{2,3},{3,2},{4,5},{5,4},{6,7},{7,6},{8,9},{9,8},{10,11... | collective-permute-start | bytes 1769480 | tf_op jit(solution)/shard_map/ppermute | solution.py:40
  106.5 27.1 %collective-permute-start.14 = (bf16[8,24,1536]{2,1,0:T(8,128)(2,1)}, bf16[8,24,1536]{2,1,0:T(8,128)(2,1)}, u32[]{:S(2)}, u32[]{:S(2)}) collective-permute-start(bf16[8,24,1536]{2,1,0:T(8,128)(2,1)} %pad_maximum_fusion.12), channel_id=1, source_target_pairs={{0,16},{8,24},{16,0},{24,8},{1,17},{9,25},{17,1},{25,9},{2,18},{10... | collective-permute-start | bytes 1769480 | tf_op jit(solution)/shard_map/ppermute | solution.py:40
  108.6 25.0 %copy-start.9 = (bf16[16,48,768]{2,1,0:T(8,128)(2,1)}, bf16[16,48,768]{2,1,0:T(8,128)(2,1)S(1)}, u32[]{:S(2)}) copy-start(bf16[16,48,768]{2,1,0:T(8,128)(2,1)S(1)} %pad_maximum_fusion.5.own_p) | copy-start | bytes 3538948
  108.6 28.9 %collective-permute-start.20 = (bf16[16,48,768]{2,1,0:T(8,128)(2,1)S(1)}, bf16[16,48,768]{2,1,0:T(8,128)(2,1)}, u32[]{:S(2)}, u32[]{:S(2)}) collective-permute-start(bf16[16,48,768]{2,1,0:T(8,128)(2,1)S(1)} %pad_maximum_fusion.5.own_p), channel_id=1, source_target_pairs={{0,8},{8,0},{16,24},{24,16},{1,9},{9,1},{17,25},{25,17},{2,10},{10... | collective-permute-start | bytes 3538952 | tf_op jit(solution)/shard_map/ppermute | solution.py:40
  111.4 26.1 %collective-permute-start.23 = (bf16[16,48,768]{2,1,0:T(8,128)(2,1)}, bf16[16,48,768]{2,1,0:T(8,128)(2,1)}, u32[]{:S(2)}, u32[]{:S(2)}) collective-permute-start(bf16[16,48,768]{2,1,0:T(8,128)(2,1)} %pad_maximum_fusion.6.own_q), channel_id=1, source_target_pairs={{0,8},{8,0},{16,24},{24,16},{1,9},{9,1},{17,25},{25,17},{2,10},{10... | collective-permute-start | bytes 3538952 | tf_op jit(solution)/shard_map/ppermute | solution.py:40
  133.6 15.3 %collective-permute-start.12 = (bf16[16,24,1536]{2,1,0:T(8,128)(2,1)}, bf16[16,24,1536]{2,1,0:T(8,128)(2,1)}, u32[]{:S(2)}, u32[]{:S(2)}) collective-permute-start(bf16[16,24,1536]{2,1,0:T(8,128)(2,1)} %pad_maximum_fusion.3.own_p), channel_id=1, source_target_pairs={{0,8},{8,0},{16,24},{24,16},{1,9},{9,1},{17,25},{25,17},{2,10},{10... | collective-permute-start | bytes 3538952 | tf_op jit(solution)/shard_map/ppermute | solution.py:40
  136.0 12.9 %collective-permute-start.15 = (bf16[16,24,1536]{2,1,0:T(8,128)(2,1)}, bf16[16,24,1536]{2,1,0:T(8,128)(2,1)}, u32[]{:S(2)}, u32[]{:S(2)}) collective-permute-start(bf16[16,24,1536]{2,1,0:T(8,128)(2,1)} %pad_maximum_fusion.4.own_q), channel_id=1, source_target_pairs={{0,8},{8,0},{16,24},{24,16},{1,9},{9,1},{17,25},{25,17},{2,10},{10... | collective-permute-start | bytes 3538952 | tf_op jit(solution)/shard_map/ppermute | solution.py:40
  136.6 12.3 %copy-start.22 = (s32[512]{0:T(512)}, s32[512]{0:T(512)S(1)}, u32[]{:S(2)}) copy-start(s32[512]{0:T(512)S(1)} %get-tuple-element.74) | copy-start | bytes 6148
  162.4 42.2 %all-to-all-start.2 = ((bf16[8,128,768]{2,1,0:T(8,128)(2,1)}), bf16[8,128,768]{2,1,0:T(8,128)(2,1)S(1)}, u32[]{:S(2)}, u32[]{:S(2)}) async-start(bf16[8,128,768]{2,1,0:T(8,128)(2,1)} %get-tuple-element.42), calls=%async_computation.2 | async-start | bytes 3145728 | tf_op jit(solution)/shard_map/all_to_all | solution.py:357
  216.4 20.8 %copy-start.26 = (f32[512,3072]{1,0:T(8,128)}, f32[512,3072]{1,0:T(8,128)S(1)}, u32[]{:S(2)}) copy-start(f32[512,3072]{1,0:T(8,128)S(1)} %fusion.68) | copy-start | bytes 18874372
  247.9 159.4 %all-to-all-start.1 = ((bf16[8,128,768]{2,1,0:T(8,128)(2,1)}), bf16[8,128,768]{2,1,0:T(8,128)(2,1)}, u32[]{:S(2)}, u32[]{:S(2)}) async-start(bf16[8,128,768]{2,1,0:T(8,128)(2,1)} %pick_tiles.9), calls=%async_computation.1 | async-start | bytes 3145728 | tf_op jit(solution)/shard_map/all_to_all | solution.py:357
  298.8 11.2 %collective-permute-start.24 = (bf16[2,2,2,2,24,1536]{5,4,2,1,3,0:T(8,128)(2,1)S(1)}, bf16[2,2,2,2,24,1536]{5,4,2,1,3,0:T(8,128)(2,1)S(1)}, u32[]{:S(2)}, u32[]{:S(2)}) collective-permute-start(bf16[2,2,2,2,24,1536]{5,4,2,1,3,0:T(8,128)(2,1)S(1)} %bitcast.346), channel_id=1, source_target_pairs={{0,8},{8,0},{16,24},{24,16},{1,9},{9,1},{17,25},{25,17},{2,10},{10... | collective-permute-start | bytes 3538952 | tf_op jit(solution)/shard_map/ppermute | solution.py:40
  300.5 16.7 %collective-permute-start.29 = (bf16[2,2,2,2,24,1664]{5,4,2,1,0,3:T(8,128)(2,1)S(1)}, bf16[2,2,2,2,24,1664]{5,4,2,1,0,3:T(8,128)(2,1)S(1)}, u32[]{:S(2)}, u32[]{:S(2)}) collective-permute-start(bf16[2,2,2,2,24,1664]{5,4,2,1,0,3:T(8,128)(2,1)S(1)} %bitcast.345), channel_id=1, source_target_pairs={{0,8},{8,0},{16,24},{24,16},{1,9},{9,1},{17,25},{25,17},{2,10},{10... | collective-permute-start | bytes 3833864 | tf_op jit(solution)/shard_map/ppermute | solution.py:40
  302.3 8.6 %collective-permute-start.39 = (bf16[2,2,2,2,24,1536]{5,4,2,1,3,0:T(8,128)(2,1)S(1)}, bf16[2,2,2,2,24,1536]{5,4,2,1,3,0:T(8,128)(2,1)S(1)}, u32[]{:S(2)}, u32[]{:S(2)}) collective-permute-start(bf16[2,2,2,2,24,1536]{5,4,2,1,3,0:T(8,128)(2,1)S(1)} %bitcast.348), channel_id=1, source_target_pairs={{0,8},{8,0},{16,24},{24,16},{1,9},{9,1},{17,25},{25,17},{2,10},{10... | collective-permute-start | bytes 3538952 | tf_op jit(solution)/shard_map/ppermute | solution.py:40
  302.7 9.2 %collective-permute-start.34 = (bf16[2,2,2,2,24,1536]{5,4,2,1,0,3:T(8,128)(2,1)S(1)}, bf16[2,2,2,2,24,1536]{5,4,2,1,0,3:T(8,128)(2,1)S(1)}, u32[]{:S(2)}, u32[]{:S(2)}) collective-permute-start(bf16[2,2,2,2,24,1536]{5,4,2,1,0,3:T(8,128)(2,1)S(1)} %bitcast.347), channel_id=1, source_target_pairs={{0,8},{8,0},{16,24},{24,16},{1,9},{9,1},{17,25},{25,17},{2,10},{10... | collective-permute-start | bytes 3538952 | tf_op jit(solution)/shard_map/ppermute | solution.py:40
  309.9 4.0 collective-permute-start.49
  310.1 6.2 %collective-permute-start.44 = (bf16[2,2,2,2,48,768]{5,4,3,2,1,0:T(8,128)(2,1)S(1)}, bf16[2,2,2,2,48,768]{5,4,3,2,1,0:T(8,128)(2,1)S(1)}, u32[]{:S(2)}, u32[]{:S(2)}) collective-permute-start(bf16[2,2,2,2,48,768]{5,4,3,2,1,0:T(8,128)(2,1)S(1)} %dynamic-slice_bitcast_fusion), channel_id=1, source_target_pairs={{0,8},{8,0},{16,24},{24,16},{1,9},{9,1},{17,25},{25,17},{2,10},{10... | collective-permute-start | bytes 3538952 | tf_op jit(solution)/shard_map/ppermute | solution.py:40
  311.0 16.3 %collective-permute-start.25 = (bf16[2,2,2,24,1536]{4,3,1,0,2:T(8,128)(2,1)S(1)}, bf16[2,2,2,24,1536]{4,3,1,0,2:T(8,128)(2,1)S(1)}, u32[]{:S(2)}, u32[]{:S(2)}) collective-permute-start(bf16[2,2,2,24,1536]{4,3,1,0,2:T(8,128)(2,1)S(1)} %dynamic-slice_bitcast_fusion.6), channel_id=1, source_target_pairs={{0,16},{8,24},{16,0},{24,8},{1,17},{9,25},{17,1},{25,9},{2,18},{10... | collective-permute-start | bytes 1769480 | tf_op jit(solution)/shard_map/ppermute | solution.py:40
  311.9 28.0 %collective-permute-start.40 = (bf16[2,2,2,24,1536]{4,3,1,0,2:T(8,128)(2,1)S(1)}, bf16[2,2,2,24,1536]{4,3,1,0,2:T(8,128)(2,1)S(1)}, u32[]{:S(2)}, u32[]{:S(2)}) collective-permute-start(bf16[2,2,2,24,1536]{4,3,1,0,2:T(8,128)(2,1)S(1)} %dynamic-slice_bitcast_fusion.4), channel_id=1, source_target_pairs={{0,16},{8,24},{16,0},{24,8},{1,17},{9,25},{17,1},{25,9},{2,18},{10... | collective-permute-start | bytes 1769480 | tf_op jit(solution)/shard_map/ppermute | solution.py:40
  313.9 28.1 %collective-permute-start.35 = (bf16[2,2,2,24,1536]{4,3,2,1,0:T(8,128)(2,1)S(1)}, bf16[2,2,2,24,1536]{4,3,2,1,0:T(8,128)(2,1)S(1)}, u32[]{:S(2)}, u32[]{:S(2)}) collective-permute-start(bf16[2,2,2,24,1536]{4,3,2,1,0:T(8,128)(2,1)S(1)} %dynamic-slice_bitcast_fusion.5), channel_id=1, source_target_pairs={{0,1},{1,0},{2,3},{3,2},{4,5},{5,4},{6,7},{7,6},{8,9},{9,8},{10,11... | collective-permute-start | bytes 1769480 | tf_op jit(solution)/shard_map/ppermute | solution.py:40
  316.3 35.3 %collective-permute-start.50 = (bf16[2,2,2,48,768]{4,3,1,0,2:T(8,128)(2,1)S(1)}, bf16[2,2,2,48,768]{4,3,1,0,2:T(8,128)(2,1)S(1)}, u32[]{:S(2)}, u32[]{:S(2)}) collective-permute-start(bf16[2,2,2,48,768]{4,3,1,0,2:T(8,128)(2,1)S(1)} %dynamic-slice_bitcast_fusion.2), channel_id=1, source_target_pairs={{0,16},{8,24},{16,0},{24,8},{1,17},{9,25},{17,1},{25,9},{2,18},{10... | collective-permute-start | bytes 1769480 | tf_op jit(solution)/shard_map/ppermute | solution.py:40
  317.2 35.1 %collective-permute-start.45 = (bf16[2,2,2,48,768]{4,3,2,1,0:T(8,128)(2,1)S(1)}, bf16[2,2,2,48,768]{4,3,2,1,0:T(8,128)(2,1)S(1)}, u32[]{:S(2)}, u32[]{:S(2)}) collective-permute-start(bf16[2,2,2,48,768]{4,3,2,1,0:T(8,128)(2,1)S(1)} %dynamic-slice_bitcast_fusion.3), channel_id=1, source_target_pairs={{0,1},{1,0},{2,3},{3,2},{4,5},{5,4},{6,7},{7,6},{8,9},{9,8},{10,11... | collective-permute-start | bytes 1769480 | tf_op jit(solution)/shard_map/ppermute | solution.py:40
  327.3 29.3 %collective-permute-start.30 = (bf16[2,2,2,24,1664]{4,3,2,1,0:T(8,128)(2,1)S(1)}, bf16[2,2,2,24,1664]{4,3,2,1,0:T(8,128)(2,1)S(1)}, u32[]{:S(2)}, u32[]{:S(2)}) collective-permute-start(bf16[2,2,2,24,1664]{4,3,2,1,0:T(8,128)(2,1)S(1)} %dynamic-slice_bitcast_fusion.1), channel_id=1, source_target_pairs={{0,1},{1,0},{2,3},{3,2},{4,5},{5,4},{6,7},{7,6},{8,9},{9,8},{10,11... | collective-permute-start | bytes 1916936 | tf_op jit(solution)/shard_map/ppermute | solution.py:40
  339.9 22.9 %collective-permute-start.26 = (bf16[2,2,24,1536]{3,2,1,0:T(8,128)(2,1)S(1)}, bf16[2,2,24,1536]{3,2,1,0:T(8,128)(2,1)S(1)}, u32[]{:S(2)}, u32[]{:S(2)}) collective-permute-start(bf16[2,2,24,1536]{3,2,1,0:T(8,128)(2,1)S(1)} %dynamic-slice_bitcast_fusion.12), channel_id=1, source_target_pairs={{0,1},{1,0},{2,3},{3,2},{4,5},{5,4},{6,7},{7,6},{8,9},{9,8},{10,11... | collective-permute-start | bytes 884744 | tf_op jit(solution)/shard_map/ppermute | solution.py:40
  342.0 27.1 %collective-permute-start.41 = (bf16[2,2,24,1536]{3,2,1,0:T(8,128)(2,1)S(1)}, bf16[2,2,24,1536]{3,2,1,0:T(8,128)(2,1)S(1)}, u32[]{:S(2)}, u32[]{:S(2)}) collective-permute-start(bf16[2,2,24,1536]{3,2,1,0:T(8,128)(2,1)S(1)} %dynamic-slice_bitcast_fusion.10), channel_id=1, source_target_pairs={{0,1},{1,0},{2,3},{3,2},{4,5},{5,4},{6,7},{7,6},{8,9},{9,8},{10,11... | collective-permute-start | bytes 884744 | tf_op jit(solution)/shard_map/ppermute | solution.py:40
  351.6 20.6 %collective-permute-start.36 = (bf16[2,2,24,1536]{3,2,1,0:T(8,128)(2,1)S(1)}, bf16[2,2,24,1536]{3,2,1,0:T(8,128)(2,1)S(1)}, u32[]{:S(2)}, u32[]{:S(2)}) collective-permute-start(bf16[2,2,24,1536]{3,2,1,0:T(8,128)(2,1)S(1)} %dynamic-slice_bitcast_fusion.11), channel_id=1, source_target_pairs={{0,16},{8,24},{16,0},{24,8},{1,17},{9,25},{17,1},{25,9},{2,18},{10... | collective-permute-start | bytes 884744 | tf_op jit(solution)/shard_map/ppermute | solution.py:40
  352.3 21.8 %collective-permute-start.51 = (bf16[2,2,48,768]{3,2,1,0:T(8,128)(2,1)S(1)}, bf16[2,2,48,768]{3,2,1,0:T(8,128)(2,1)S(1)}, u32[]{:S(2)}, u32[]{:S(2)}) collective-permute-start(bf16[2,2,48,768]{3,2,1,0:T(8,128)(2,1)S(1)} %dynamic-slice_bitcast_fusion.8), channel_id=1, source_target_pairs={{0,1},{1,0},{2,3},{3,2},{4,5},{5,4},{6,7},{7,6},{8,9},{9,8},{10,11... | collective-permute-start | bytes 884744 | tf_op jit(solution)/shard_map/ppermute | solution.py:40
  356.5 20.6 %collective-permute-start.46 = (bf16[2,2,48,768]{3,2,1,0:T(8,128)(2,1)S(1)}, bf16[2,2,48,768]{3,2,1,0:T(8,128)(2,1)S(1)}, u32[]{:S(2)}, u32[]{:S(2)}) collective-permute-start(bf16[2,2,48,768]{3,2,1,0:T(8,128)(2,1)S(1)} %dynamic-slice_bitcast_fusion.9), channel_id=1, source_target_pairs={{0,16},{8,24},{16,0},{24,8},{1,17},{9,25},{17,1},{25,9},{2,18},{10... | collective-permute-start | bytes 884744 | tf_op jit(solution)/shard_map/ppermute | solution.py:40
  362.8 39.8 %collective-permute-start.31 = (bf16[2,2,24,1664]{3,2,1,0:T(8,128)(2,1)S(1)}, bf16[2,2,24,1664]{3,2,1,0:T(8,128)(2,1)S(1)}, u32[]{:S(2)}, u32[]{:S(2)}) collective-permute-start(bf16[2,2,24,1664]{3,2,1,0:T(8,128)(2,1)S(1)} %dynamic-slice_bitcast_fusion.7), channel_id=1, source_target_pairs={{0,16},{8,24},{16,0},{24,8},{1,17},{9,25},{17,1},{25,9},{2,18},{10... | collective-permute-start | bytes 958472 | tf_op jit(solution)/shard_map/ppermute | solution.py:40
  369.1 18.6 %collective-permute-start.27 = (bf16[2,24,1536]{2,1,0:T(8,128)(2,1)S(1)}, bf16[2,24,1536]{2,1,0:T(8,128)(2,1)S(1)}, u32[]{:S(2)}, u32[]{:S(2)}) collective-permute-start(bf16[2,24,1536]{2,1,0:T(8,128)(2,1)S(1)} %dynamic-slice_bitcast_fusion.18), channel_id=1, source_target_pairs={{0,4},{1,5},{2,6},{3,7},{4,0},{5,1},{6,2},{7,3},{8,12},{9,13},{10,... | collective-permute-start | bytes 442376 | tf_op jit(solution)/shard_map/ppermute | solution.py:40
  372.2 18.7 %collective-permute-start.42 = (bf16[2,24,1536]{2,1,0:T(8,128)(2,1)S(1)}, bf16[2,24,1536]{2,1,0:T(8,128)(2,1)S(1)}, u32[]{:S(2)}, u32[]{:S(2)}) collective-permute-start(bf16[2,24,1536]{2,1,0:T(8,128)(2,1)S(1)} %dynamic-slice_bitcast_fusion.16), channel_id=1, source_target_pairs={{0,4},{1,5},{2,6},{3,7},{4,0},{5,1},{6,2},{7,3},{8,12},{9,13},{10,... | collective-permute-start | bytes 442376 | tf_op jit(solution)/shard_map/ppermute | solution.py:40
  374.1 23.1 %collective-permute-start.37 = (bf16[2,24,1536]{2,1,0:T(8,128)(2,1)S(1)}, bf16[2,24,1536]{2,1,0:T(8,128)(2,1)S(1)}, u32[]{:S(2)}, u32[]{:S(2)}) collective-permute-start(bf16[2,24,1536]{2,1,0:T(8,128)(2,1)S(1)} %dynamic-slice_bitcast_fusion.17), channel_id=1, source_target_pairs={{0,4},{1,5},{2,6},{3,7},{4,0},{5,1},{6,2},{7,3},{8,12},{9,13},{10,... | collective-permute-start | bytes 442376 | tf_op jit(solution)/shard_map/ppermute | solution.py:40
  377.1 23.3 %collective-permute-start.52 = (bf16[2,48,768]{2,1,0:T(8,128)(2,1)S(1)}, bf16[2,48,768]{2,1,0:T(8,128)(2,1)S(1)}, u32[]{:S(2)}, u32[]{:S(2)}) collective-permute-start(bf16[2,48,768]{2,1,0:T(8,128)(2,1)S(1)} %dynamic-slice_bitcast_fusion.14), channel_id=1, source_target_pairs={{0,4},{1,5},{2,6},{3,7},{4,0},{5,1},{6,2},{7,3},{8,12},{9,13},{10,... | collective-permute-start | bytes 442376 | tf_op jit(solution)/shard_map/ppermute | solution.py:40
  387.7 14.2 %collective-permute-start.47 = (bf16[2,48,768]{2,1,0:T(8,128)(2,1)S(1)}, bf16[2,48,768]{2,1,0:T(8,128)(2,1)S(1)}, u32[]{:S(2)}, u32[]{:S(2)}) collective-permute-start(bf16[2,48,768]{2,1,0:T(8,128)(2,1)S(1)} %dynamic-slice_bitcast_fusion.15), channel_id=1, source_target_pairs={{0,4},{1,5},{2,6},{3,7},{4,0},{5,1},{6,2},{7,3},{8,12},{9,13},{10,... | collective-permute-start | bytes 442376 | tf_op jit(solution)/shard_map/ppermute | solution.py:40
  390.9 22.1 %collective-permute-start.28 = (bf16[24,1536]{1,0:T(8,128)(2,1)S(1)}, bf16[24,1536]{1,0:T(8,128)(2,1)S(1)}, u32[]{:S(2)}, u32[]{:S(2)}) collective-permute-start(bf16[24,1536]{1,0:T(8,128)(2,1)S(1)} %dynamic-slice_bitcast_fusion.24), channel_id=1, source_target_pairs={{0,2},{1,3},{2,0},{3,1},{4,6},{5,7},{6,4},{7,5},{8,10},{9,11},{10,... | collective-permute-start | bytes 221192 | tf_op jit(solution)/shard_map/ppermute | solution.py:40
  397.3 7.6 %collective-permute-start.43 = (bf16[24,1536]{1,0:T(8,128)(2,1)S(1)}, bf16[24,1536]{1,0:T(8,128)(2,1)S(1)}, u32[]{:S(2)}, u32[]{:S(2)}) collective-permute-start(bf16[24,1536]{1,0:T(8,128)(2,1)S(1)} %dynamic-slice_bitcast_fusion.22), channel_id=1, source_target_pairs={{0,2},{1,3},{2,0},{3,1},{4,6},{5,7},{6,4},{7,5},{8,10},{9,11},{10,... | collective-permute-start | bytes 221192 | tf_op jit(solution)/shard_map/ppermute | solution.py:40
  400.4 6.1 %collective-permute-start.38 = (bf16[24,1536]{1,0:T(8,128)(2,1)S(1)}, bf16[24,1536]{1,0:T(8,128)(2,1)S(1)}, u32[]{:S(2)}, u32[]{:S(2)}) collective-permute-start(bf16[24,1536]{1,0:T(8,128)(2,1)S(1)} %dynamic-slice_bitcast_fusion.23), channel_id=1, source_target_pairs={{0,2},{1,3},{2,0},{3,1},{4,6},{5,7},{6,4},{7,5},{8,10},{9,11},{10,... | collective-permute-start | bytes 221192 | tf_op jit(solution)/shard_map/ppermute | solution.py:40
  401.9 10.9 %collective-permute-start.53 = (bf16[48,768]{1,0:T(8,128)(2,1)S(1)}, bf16[48,768]{1,0:T(8,128)(2,1)S(1)}, u32[]{:S(2)}, u32[]{:S(2)}) collective-permute-start(bf16[48,768]{1,0:T(8,128)(2,1)S(1)} %dynamic-slice_bitcast_fusion.20), channel_id=1, source_target_pairs={{0,2},{1,3},{2,0},{3,1},{4,6},{5,7},{6,4},{7,5},{8,10},{9,11},{10,... | collective-permute-start | bytes 221192 | tf_op jit(solution)/shard_map/ppermute | solution.py:40
  402.6 10.3 %collective-permute-start.48 = (bf16[48,768]{1,0:T(8,128)(2,1)S(1)}, bf16[48,768]{1,0:T(8,128)(2,1)S(1)}, u32[]{:S(2)}, u32[]{:S(2)}) collective-permute-start(bf16[48,768]{1,0:T(8,128)(2,1)S(1)} %dynamic-slice_bitcast_fusion.21), channel_id=1, source_target_pairs={{0,2},{1,3},{2,0},{3,1},{4,6},{5,7},{6,4},{7,5},{8,10},{9,11},{10,... | collective-permute-start | bytes 221192 | tf_op jit(solution)/shard_map/ppermute | solution.py:40
  404.9 10.1 %collective-permute-start.32 = (bf16[2,24,1664]{2,1,0:T(8,128)(2,1)S(1)}, bf16[2,24,1664]{2,1,0:T(8,128)(2,1)S(1)}, u32[]{:S(2)}, u32[]{:S(2)}) collective-permute-start(bf16[2,24,1664]{2,1,0:T(8,128)(2,1)S(1)} %dynamic-slice_bitcast_fusion.13), channel_id=1, source_target_pairs={{0,4},{1,5},{2,6},{3,7},{4,0},{5,1},{6,2},{7,3},{8,12},{9,13},{10,... | collective-permute-start | bytes 479240 | tf_op jit(solution)/shard_map/ppermute | solution.py:40
  407.2 42.7 %all-to-all-start.3 = ((bf16[8,128,768]{2,1,0:T(8,128)(2,1)}), bf16[8,128,768]{2,1,0:T(8,128)(2,1)S(1)}, u32[]{:S(2)}, u32[]{:S(2)}) async-start(bf16[8,128,768]{2,1,0:T(8,128)(2,1)} %pick_tiles.12), calls=%async_computation.3 | async-start | bytes 3145728 | tf_op jit(solution)/shard_map/all_to_all | solution.py:357
  415.1 25.9 %collective-permute-start.33 = (bf16[24,1664]{1,0:T(8,128)(2,1)S(1)}, bf16[24,1664]{1,0:T(8,128)(2,1)S(1)}, u32[]{:S(2)}, u32[]{:S(2)}) collective-permute-start(bf16[24,1664]{1,0:T(8,128)(2,1)S(1)} %dynamic-slice_bitcast_fusion.19), channel_id=1, source_target_pairs={{0,2},{1,3},{2,0},{3,1},{4,6},{5,7},{6,4},{7,5},{8,10},{9,11},{10,... | collective-permute-start | bytes 239624 | tf_op jit(solution)/shard_map/ppermute | solution.py:40
  (30 other events, 104.5 us)
